TPU v7x, 256 devices: a whole 4x4x8 slice. The times are simulated.
256 devices in a mesh: pipe: 4 (over y), dp: 4 (over x), expert: 16 (over z, core).
Axes of the slice: x: 4, y: 4, z: 8, core: 2. Of those that a mesh axis runs over, the one named last changes fastest.
Arguments:
- block_input: bfloat16 [4, 8192, 3072], P('pipe', ('dp', 'expert')), may hold values from -6 to 6
- output_grad: bfloat16 [4, 8192, 3072], P('pipe', ('dp', 'expert')), may hold values from -6 to 6
- expert_ids: int32 [4, 8192, 6], P('pipe', ('dp', 'expert')), may hold values from 0 to 159, all different within a row
- gate_weights: float32 [4, 8192, 6], P('pipe', ('dp', 'expert')), may hold values from 0.25 to 2
- gate_proj: bfloat16 [4, 16, 3072, 1024], P('pipe', 'expert', None, 'dp'), may hold values from -0.109375 to 0.109375
- up_proj: bfloat16 [4, 16, 3072, 1024], P('pipe', 'expert', None, 'dp'), may hold values from -0.109375 to 0.109375
- down_proj: bfloat16 [4, 16, 1024, 3072], P('pipe', 'expert', 'dp'), may hold values from -0.1875 to 0.1875
Outputs:
- received_grad: bfloat16 [4, 8192, 3072], P('pipe', ('dp', 'expert'))
- gate_weight_grad: float32 [4, 8192, 6], P('pipe', ('dp', 'expert'))
- gate_proj_grad: bfloat16 [4, 16, 3072, 1024], P('pipe', 'expert', None, 'dp')
- up_proj_grad: bfloat16 [4, 16, 3072, 1024], P('pipe', 'expert', None, 'dp')
- down_proj_grad: bfloat16 [4, 16, 1024, 3072], P('pipe', 'expert', 'dp')
Inputs may be any that keep to these rules, and one draw needn't show every extreme that they name: `expert_ids`: each token names 6 different experts.
All inputs are finite; a program needn't handle non-finite values.
Results may differ from a plain program's by a relative error of at most 0.006.
Values may be sent and summed in bfloat16 or wider, within the bound.
A program may use at most 128 MiB of HBM per device.

v0:
```python
import jax
import jax.numpy as jnp
from jax import lax
from jax.sharding import PartitionSpec as P


def shifted(value, axis, steps):
    count = lax.axis_size(axis)
    pairs = [(source, (source + steps) % count) for source in range(count)]
    return lax.ppermute(value, axis, pairs)


def slot_tables(chosen_ids, experts, capacity):
    tok_count, chosen = chosen_ids.shape
    flat_ids = chosen_ids.reshape(-1)
    columns = jnp.arange(experts, dtype=jnp.int32)
    onehot = (flat_ids[:, None] == columns[None, :]).astype(jnp.int32)
    earlier = jnp.cumsum(onehot, axis=0) - onehot
    slot_rank = jnp.sum(earlier * onehot, axis=1)
    kept_pair = (flat_ids < experts) & (slot_rank < capacity)
    slot_index = jnp.where(kept_pair, flat_ids * capacity + slot_rank, experts * capacity)
    slot_rows = jnp.arange(experts * capacity, dtype=jnp.int32)
    placed = slot_index[None, :] == slot_rows[:, None]
    pair_index = jnp.arange(tok_count * chosen, dtype=jnp.int32)
    source_pair = jnp.sum(jnp.where(placed, pair_index[None, :], 0), axis=1)
    filled = jnp.any(placed, axis=1)
    return (slot_index, source_pair, filled)


def shards(block_input, output_grad, expert_ids, gate_weights, gate_proj, up_proj, down_proj):
    acts_local = block_input[0]
    grad_local = output_grad[0]
    chosen_ids = expert_ids[0]
    route_weight = gate_weights[0]
    tok_count, chosen = chosen_ids.shape
    width = acts_local.shape[1]
    local_count = gate_proj.shape[1]
    dp_count = lax.axis_size("dp")
    expert_count = lax.axis_size("expert")
    experts = local_count * expert_count
    capacity = tok_count // 16
    slot_index, source_pair, filled = slot_tables(chosen_ids, experts, capacity)
    source_token = source_pair // chosen
    slot_weight = route_weight.reshape(-1)[source_pair]
    send_acts = jnp.where(filled[:, None], acts_local[source_token], jnp.zeros((), jnp.bfloat16))
    scaled = slot_weight[:, None] * grad_local[source_token].astype(jnp.float32)
    send_grad = jnp.where(filled[:, None], scaled, 0.0).astype(jnp.bfloat16)
    send_acts = send_acts.reshape(experts, capacity, width)
    send_grad = send_grad.reshape(experts, capacity, width)
    acts_copies = jnp.broadcast_to(send_acts[None], (dp_count,) + send_acts.shape).reshape(
        dp_count * experts, capacity, width
    )
    grad_copies = jnp.broadcast_to(send_grad[None], (dp_count,) + send_grad.shape).reshape(
        dp_count * experts, capacity, width
    )
    recv_acts, recv_grad = (
        lax.all_to_all(acts_copies, ("dp", "expert"), split_axis=0, concat_axis=1, tiled=True),
        lax.all_to_all(grad_copies, ("dp", "expert"), split_axis=0, concat_axis=1, tiled=True),
    )
    gate_local = gate_proj[0]
    upper_local = up_proj[0]
    lower_local = down_proj[0]
    gate_pre = jnp.einsum("erd,edh->erh", recv_acts, gate_local, preferred_element_type=jnp.float32)
    up_value = jnp.einsum(
        "erd,edh->erh", recv_acts, upper_local, preferred_element_type=jnp.float32
    )
    grad_hidden = jnp.einsum(
        "erd,ehd->erh", recv_grad, lower_local, preferred_element_type=jnp.float32
    )
    sigma_gate = jax.nn.sigmoid(gate_pre)
    swish = gate_pre * sigma_gate
    hidden = swish * up_value
    scores = jnp.sum(hidden * grad_hidden, axis=2)
    lower_grad = jnp.einsum(
        "erh,erd->ehd", hidden.astype(jnp.bfloat16), recv_grad, preferred_element_type=jnp.float32
    ).astype(jnp.bfloat16)
    delta_gate = (
        grad_hidden * up_value * sigma_gate * (1.0 + gate_pre * (1.0 - sigma_gate))
    ).astype(jnp.bfloat16)
    delta_up = (grad_hidden * swish).astype(jnp.bfloat16)
    gate_grad = jnp.einsum(
        "erd,erh->edh", recv_acts, delta_gate, preferred_element_type=jnp.float32
    ).astype(jnp.bfloat16)
    upper_grad = jnp.einsum(
        "erd,erh->edh", recv_acts, delta_up, preferred_element_type=jnp.float32
    ).astype(jnp.bfloat16)
    partial_value = jnp.einsum(
        "erh,edh->erd", delta_gate, gate_local, preferred_element_type=jnp.float32
    ) + jnp.einsum("erh,edh->erd", delta_up, upper_local, preferred_element_type=jnp.float32)
    back_rows, back_scores = (
        lax.all_to_all(partial_value, ("dp", "expert"), split_axis=1, concat_axis=0, tiled=True),
        lax.all_to_all(scores, ("dp", "expert"), split_axis=1, concat_axis=0, tiled=True),
    )
    slot_grad = jnp.sum(back_rows.reshape(dp_count, experts * capacity, width), axis=0).astype(
        jnp.bfloat16
    )
    slot_scores = jnp.sum(back_scores.reshape(dp_count, experts * capacity), axis=0)
    token_rows = jnp.arange(tok_count, dtype=jnp.int32)
    token_map = ((source_token[:, None] == token_rows[None, :]) & filled[:, None]).astype(
        jnp.bfloat16
    )
    input_grad = jnp.einsum(
        "st,sd->td", token_map, slot_grad, preferred_element_type=jnp.float32
    ).astype(jnp.bfloat16)
    padded_scores = jnp.concatenate([slot_scores, jnp.zeros((1,), jnp.float32)])
    weight_grad = (padded_scores[slot_index] / route_weight.reshape(-1)).reshape(tok_count, chosen)
    received = shifted(input_grad, "pipe", -1)
    return (received[None], weight_grad[None], gate_grad[None], upper_grad[None], lower_grad[None])


def solution(mesh):
    in_specs = (
        P("pipe", ("dp", "expert"), None),
        P("pipe", ("dp", "expert"), None),
        P("pipe", ("dp", "expert"), None),
        P("pipe", ("dp", "expert"), None),
        P("pipe", "expert", None, "dp"),
        P("pipe", "expert", None, "dp"),
        P("pipe", "expert", "dp", None),
    )
    out_specs = (
        P("pipe", ("dp", "expert"), None),
        P("pipe", ("dp", "expert"), None),
        P("pipe", "expert", None, "dp"),
        P("pipe", "expert", None, "dp"),
        P("pipe", "expert", "dp", None),
    )
    return jax.shard_map(shards, mesh=mesh, in_specs=in_specs, out_specs=out_specs, check_vma=False)
```

profile of v0, /device:TPU:1, one launch (start us, length us, event | category | flops | bytes accessed | tf_op | source)
XLA Modules:
  0.0 386.8 jit_solution(3359856980228247124)
XLA Ops:
  0.6 0.0 copy-start
  0.6 0.9 copy.30
  1.6 0.1 reshape_squeeze.7
  1.7 0.1 eq.52
  1.8 1.7 reduce-window.6
  3.6 0.3 slice_reduce_fusion
  3.8 0.1 fusion.29
  4.0 0.1 fusion.22
  4.1 0.1 select_reduce_fusion
  4.2 0.1 broadcast_in_dim.81
  4.3 3.1 gather_fusion.2
  7.4 0.1 bitcast_select_fusion
  7.6 2.1 broadcast_in_dim.86
  9.6 13.3 %all-to-all-start.1 = ((bf16[64,8,3072]{2,1,0:T(8,128)(2,1)}), bf16[64,8,3072]{2,1,0:T(8,128)(2,1)}, u32[]{:S(2)}, u32[]{:S(2)}) async-start(bf16[64,8,3072]{2,1,0:T(8,128)(2,1)} %bitcast.95), calls=%async_computation.1 | async-start | bytes 6291456 | tf_op jit(solution)/shard_map/all_to_all | solution.py:57
  22.9 0.0 copy-done.6
  22.9 0.1 copy.33
  23.0 0.1 reshape_squeeze.8
  23.2 1.0 gather_fusion
  24.1 0.1 mul.70
  24.2 0.0 copy-done.1
  24.2 1.0 gather_fusion.1
  25.3 0.3 fusion.13
  25.6 70.8 %all-to-all-done.1 = bf16[64,8,3072]{2,1,0:T(8,128)(2,1)} async-done(((bf16[64,8,3072]{2,1,0:T(8,128)(2,1)}), bf16[64,8,3072]{2,1,0:T(8,128)(2,1)}, u32[]{:S(2)}, u32[]{:S(2)}) %all-to-all-start.1) | async-done | bytes 3145760 | tf_op jit(solution)/shard_map/all_to_all | solution.py:57
  96.3 2.1 broadcast_in_dim.84
  98.4 6.3 %all-to-all-start = ((bf16[64,8,3072]{2,1,0:T(8,128)(2,1)}), bf16[64,8,3072]{2,1,0:T(8,128)(2,1)}, u32[]{:S(2)}, u32[]{:S(2)}) async-start(bf16[64,8,3072]{2,1,0:T(8,128)(2,1)} %bitcast.96), calls=%async_computation | async-start | bytes 6291456 | tf_op jit(solution)/shard_map/all_to_all | solution.py:58
  104.7 0.0 copy-done
  104.7 0.0 copy-start.2
  104.7 3.8 fusion.5
  108.6 0.0 copy-done.2
  108.6 3.7 fusion.7
  112.3 65.9 %all-to-all-done = bf16[64,8,3072]{2,1,0:T(8,128)(2,1)} async-done(((bf16[64,8,3072]{2,1,0:T(8,128)(2,1)}), bf16[64,8,3072]{2,1,0:T(8,128)(2,1)}, u32[]{:S(2)}, u32[]{:S(2)}) %all-to-all-start) | async-done | bytes 3145760 | tf_op jit(solution)/shard_map/all_to_all | solution.py:58
  178.1 3.8 multiply_reduce_fusion
  181.9 0.0 copy-start.3
  182.0 1.0 fusion.14
  183.0 0.0 copy-done.3
  183.0 1.0 add_bitcast_fusion
  184.0 19.1 %copy.34 = f32[1,512,3072]{2,0,1:T(1,128)} copy(f32[1,512,3072]{2,1,0:T(8,128)S(1)} %add_bitcast_fusion) | data formatting | bytes 12582912 | tf_op jit(solution)/shard_map/add | solution.py:87
  203.1 6.4 %all-to-all-start.2 = ((f32[1,512,3072]{2,0,1:T(1,128)}), f32[1,512,3072]{2,0,1:T(1,128)}, u32[]{:S(2)}, u32[]{:S(2)}) async-start(f32[1,512,3072]{2,0,1:T(1,128)} %copy.34), calls=%async_computation.2 | async-start | bytes 12582912 | tf_op jit(solution)/shard_map/all_to_all | solution.py:91
  209.5 0.0 copy-done.5
  209.5 0.1 copy.36
  209.7 0.1 lt.81
  209.8 0.1 copy.37
  210.0 0.1 mul.82
  210.2 0.7 all_to_all.14
  210.9 4.1 %fusion = bf16[1,1,3072,256]{3,2,1,0:T(8,128)(2,1)} fusion(bf16[512,256]{0,1:T(8,128)(2,1)S(1)} %get-tuple-element.21, bf16[64,8,3072]{2,1,0:T(8,128)(2,1)} %all-to-all-done.1), kind=kOutput, calls=%fused_computation.8 | convolution fusion | flops 806092800 | bytes 4980736 | tf_op jit(solution)/shard_map/erd,erh->edh/dot_general | solution.py:81
  214.9 135.4 %all-to-all-done.2 = f32[1,512,3072]{2,0,1:T(1,128)} async-done(((f32[1,512,3072]{2,0,1:T(1,128)}), f32[1,512,3072]{2,0,1:T(1,128)}, u32[]{:S(2)}, u32[]{:S(2)}) %all-to-all-start.2) | async-done | bytes 6291488 | tf_op jit(solution)/shard_map/all_to_all | solution.py:91
  350.4 5.8 %all-to-all-start.3 = ((f32[1,64,8]{2,0,1:T(1,128)}), f32[1,64,8]{2,0,1:T(1,128)S(1)}, u32[]{:S(2)}, u32[]{:S(2)}) async-start(f32[1,64,8]{2,0,1:T(1,128)} %bitcast.17), calls=%async_computation.3 | async-start | bytes 65536 | tf_op jit(solution)/shard_map/all_to_all | solution.py:92
  356.2 6.8 %copy.40 = f32[1,512,3072]{2,1,0:T(8,128)} copy(f32[1,512,3072]{2,0,1:T(1,128)} %all-to-all-done.2) | data formatting | bytes 12582912
  363.0 3.4 reduce_sum.52
  366.4 0.5 convolution_convert_fusion.3
  366.9 0.0 copy-start.4
  366.9 2.8 collective-permute-start
  369.7 4.4 %fusion.2 = bf16[1,1,256,3072]{3,2,1,0:T(8,128)(2,1)} fusion(bf16[64,8,3072]{2,1,0:T(8,128)(2,1)} %all-to-all-done, f32[512,256]{0,1:T(8,128)} %fusion.7, f32[512,256]{0,1:T(8,128)} %fusion.5), kind=kOutput, calls=%fused_computation.10 | convolution fusion | flops 806879232 | bytes 5767168 | tf_op jit(solution)/shard_map/erh,erd->ehd/dot_general | solution.py:74
  374.1 0.0 copy-done.4
  374.1 4.1 %fusion.1 = bf16[1,1,3072,256]{3,2,1,0:T(8,128)(2,1)} fusion(bf16[512,256]{0,1:T(8,128)(2,1)S(1)} %copy-done.4, bf16[64,8,3072]{2,1,0:T(8,128)(2,1)} %all-to-all-done.1), kind=kOutput, calls=%fused_computation.9 | convolution fusion | flops 806092800 | bytes 4980736 | tf_op jit(solution)/shard_map/erd,erh->edh/dot_general | solution.py:84
  378.2 0.0 all-to-all-done.3
  378.2 0.5 broadcast.241
  378.7 0.7 reduce.9
  379.4 0.1 reshape.293
  379.5 5.0 %gather_fusion.3 = f32[768]{0:T(1024)S(1)} fusion(f32[129]{0:T(256)S(1)} %pad_maximum_fusion, s32[1024]{0:T(1024)S(1)} %pad_clamp_fusion), kind=kCustom, calls=%fused_computation.3 | custom fusion | bytes 9216 | tf_op jit(solution)/shard_map/gather | solution.py:106
  384.5 0.1 gather.21
  384.7 0.7 copy.39
  385.3 0.6 collective-permute-done
  385.9 0.9 copy.44
  (16 shorter events, 0.2 us)
Async XLA Ops:
  0.6 104.1 %copy-start = (bf16[1,1,3072,256]{3,2,1,0:T(8,128)(2,1)S(1)}, bf16[1,1,3072,256]{3,2,1,0:T(8,128)(2,1)}, u32[]{:S(2)}) copy-start(bf16[1,1,3072,256]{3,2,1,0:T(8,128)(2,1)} %param.11) | copy-start | bytes 4718596
  9.6 13.3 %copy-start.6 = (f32[1,128,6]{1,0,2:T(1,128)S(1)}, f32[1,128,6]{1,0,2:T(1,128)}, u32[]{:S(2)}) copy-start(f32[1,128,6]{1,0,2:T(1,128)} %param.10) | copy-start | bytes 9220
  9.6 14.6 %copy-start.1 = (bf16[1,128,3072]{2,1,0:T(8,128)(2,1)S(1)}, bf16[1,128,3072]{2,1,0:T(8,128)(2,1)}, u32[]{:S(2)}) copy-start(bf16[1,128,3072]{2,1,0:T(8,128)(2,1)} %param.8) | copy-start | bytes 2359300
  9.6 86.7 %all-to-all-start.1 = ((bf16[64,8,3072]{2,1,0:T(8,128)(2,1)}), bf16[64,8,3072]{2,1,0:T(8,128)(2,1)}, u32[]{:S(2)}, u32[]{:S(2)}) async-start(bf16[64,8,3072]{2,1,0:T(8,128)(2,1)} %bitcast.95), calls=%async_computation.1 | async-start | bytes 6291456 | tf_op jit(solution)/shard_map/all_to_all | solution.py:57
  98.4 79.7 %all-to-all-start = ((bf16[64,8,3072]{2,1,0:T(8,128)(2,1)}), bf16[64,8,3072]{2,1,0:T(8,128)(2,1)}, u32[]{:S(2)}, u32[]{:S(2)}) async-start(bf16[64,8,3072]{2,1,0:T(8,128)(2,1)} %bitcast.96), calls=%async_computation | async-start | bytes 6291456 | tf_op jit(solution)/shard_map/all_to_all | solution.py:58
  104.7 3.8 copy-start.2
  181.9 1.1 copy-start.3
  203.1 6.4 %copy-start.5 = (s32[1,128,6]{1,0,2:T(1,128)S(1)}, s32[1,128,6]{1,0,2:T(1,128)}, u32[]{:S(2)}) copy-start(s32[1,128,6]{1,0,2:T(1,128)} %param.9) | copy-start | bytes 9220
  203.1 147.2 %all-to-all-start.2 = ((f32[1,512,3072]{2,0,1:T(1,128)}), f32[1,512,3072]{2,0,1:T(1,128)}, u32[]{:S(2)}, u32[]{:S(2)}) async-start(f32[1,512,3072]{2,0,1:T(1,128)} %copy.34), calls=%async_computation.2 | async-start | bytes 12582912 | tf_op jit(solution)/shard_map/all_to_all | solution.py:91
  350.4 27.8 %all-to-all-start.3 = ((f32[1,64,8]{2,0,1:T(1,128)}), f32[1,64,8]{2,0,1:T(1,128)S(1)}, u32[]{:S(2)}, u32[]{:S(2)}) async-start(f32[1,64,8]{2,0,1:T(1,128)} %bitcast.17), calls=%async_computation.3 | async-start | bytes 65536 | tf_op jit(solution)/shard_map/all_to_all | solution.py:92
  366.9 7.2 %copy-start.4 = (bf16[512,256]{0,1:T(8,128)(2,1)S(1)}, bf16[512,256]{0,1:T(8,128)(2,1)}, u32[]{:S(2)}) copy-start(bf16[512,256]{0,1:T(8,128)(2,1)} %copy-done.3) | copy-start | bytes 786436
  366.9 19.0 %collective-permute-start = (bf16[128,3072]{1,0:T(8,128)(2,1)S(1)}, bf16[128,3072]{1,0:T(8,128)(2,1)S(1)}, u32[]{:S(2)}, u32[]{:S(2)}) collective-permute-start(bf16[128,3072]{1,0:T(8,128)(2,1)S(1)} %convolution_convert_fusion.3), channel_id=1, source_target_pairs={{0,192},{64,0},{128,64},{192,128},{1,193},{65,1},{129,65},{193,129... | collective-permute-start | bytes 2359304 | tf_op jit(solution)/shard_map/ppermute | solution.py:10
where the time goes:
time: 389 us; the launch traced here: 387 us
  waiting for transfers between devices  273 us (70%)
  local copies, waits for them, and re-layouts  45.5 us (12%)
  starting transfers between devices  34.5 us (9%)
  matrix products  26.4 us (7%)
  other arithmetic  6.77 us (2%)
    all_to_all x1, waiting for transfers between devices, shards(): lax.all_to_all(partial_value, ('dp', 'expert'), split_axis=1, concat_axis...  135 us
    all_to_all x1, waiting for transfers between devices, shards(): lax.all_to_all(acts_copies, ('dp', 'expert'), split_axis=0, concat_axis=1...  70.8 us
    all_to_all x1, waiting for transfers between devices, shards(): lax.all_to_all(grad_copies, ('dp', 'expert'), split_axis=0, concat_axis=1...  65.9 us
    add x1, local copies, waits for them, and re-layouts, shards(): jnp.einsum('erh,edh->erd', delta_gate, gate_local, preferred_element_type...  19.1 us
    all_to_all x1, starting transfers between devices, shards(): lax.all_to_all(acts_copies, ('dp', 'expert'), split_axis=0, concat_axis=1...  13.3 us
    unnamed x19, local copies, waits for them, and re-layouts  9.41 us
  transfers between devices with their start and end apart: 5, of which 4 were waited for; matrix products, arithmetic and copies ran while one was open for 11% of the time, Pallas kernels for 0%

commit v1 on v0

v1 whole, which is shorter than its diff:
```python
import functools
import jax
import jax.numpy as jnp
from jax import lax
from jax.experimental import pallas as pl
from jax.experimental.pallas import tpu as pltpu
from jax.sharding import PartitionSpec as P

MESH = pl.DeviceIdType.MESH
CAP = 8
F32 = jnp.float32
BF16 = jnp.bfloat16
VMEM_LIMIT = 58 << 20
Z_ORDER = (0, 1, -1, 2, -2, 3, -3, 4)


def mod(value, count):
    return lax.rem(value + count, count)


def place():
    return lax.axis_index("pipe"), lax.axis_index("dp"), lax.axis_index("expert")


def remote(src, dst, send_sem, recv_sem, device):
    return pltpu.make_async_remote_copy(
        src_ref=src, dst_ref=dst, send_sem=send_sem, recv_sem=recv_sem,
        device_id=device, device_id_type=MESH)


def eight(row):
    return pl.ds(pl.multiple_of(row, 8), 8)


def slot_maps(ids_ref, slots, tokens):
    slot = lax.broadcasted_iota(jnp.int32, (slots, tokens), 0)
    expert = lax.shift_right_logical(slot, 3)
    rank = jnp.bitwise_and(slot, 7)
    return expert, rank


def fwd_kernel(nd, ne, x_ref, dy_ref, ids_ref, w_ref, rx, rg, sx, sg, smap_ref,
               xv, gv, lsem, zs, zr, xs, xr, fs, fr):
    p, i, e = place()
    z, c = e // 2, e % 2
    nz = ne // 2
    right, left = (p, mod(i + 1, nd), e), (p, mod(i - 1, nd), e)
    tokens, _ = x_ref.shape
    slots = ne * CAP
    chosen = ids_ref.shape[0]

    barrier = pltpu.get_barrier_semaphore()
    for d in range(1, ne):
        pl.semaphore_signal(barrier, inc=1, device_id=(p, i, lax.rem(e + d, ne)), device_id_type=MESH)
    for peer in (right, left):
        pl.semaphore_signal(barrier, inc=1, device_id=peer, device_id_type=MESH)

    expert, rank_of = slot_maps(ids_ref, slots, tokens)
    hit = jnp.zeros((slots, tokens), F32)
    weight = jnp.zeros((slots, tokens), F32)
    for k in range(chosen):
        same = ids_ref[k] == expert
        hit = jnp.where(same, 1.0, hit)
        weight = jnp.where(same, w_ref[k], weight)
    before = (lax.broadcasted_iota(jnp.int32, (tokens, tokens), 0)
              < lax.broadcasted_iota(jnp.int32, (tokens, tokens), 1))
    rank = jnp.dot(hit.astype(BF16), jnp.where(before, 1.0, 0.0).astype(BF16), preferred_element_type=F32)
    table = jnp.where(rank == rank_of.astype(F32), hit, 0.0)
    slot_weight = jnp.sum(table * weight, axis=1, keepdims=True)
    table = table.astype(BF16)
    smap_ref[...] = table
    xv[...] = jnp.dot(table, x_ref[...], preferred_element_type=F32).astype(BF16)
    gv[...] = (slot_weight * jnp.dot(table, dy_ref[...], preferred_element_type=F32)).astype(BF16)
    send, recv = (sx, sg), (rx, rg)
    stage = [pltpu.make_async_copy(xv, sx, lsem.at[0]), pltpu.make_async_copy(gv, sg, lsem.at[1])]
    for copy in stage:
        copy.start()
    for copy in stage:
        copy.wait()
    pl.semaphore_wait(barrier, ne - 1 + 2)

    def z_copy(kind, dz, dc):
        n = (dz % nz) * 2 + dc
        target = mod(z + dz, nz) * 2 + (c + dc - 2 * c * dc)
        return remote(send[kind].at[eight(target * CAP)], recv[kind].at[eight((i * ne + e) * CAP)],
                      zs.at[kind, n], zr.at[kind, n], (p, i, target))

    def own(kind):
        return pltpu.make_async_copy(send[kind].at[eight(e * CAP)], recv[kind].at[eight((i * ne + e) * CAP)],
                                     lsem.at[2 + kind])

    def group_rows(dp, g):
        chip = mod(z - Z_ORDER[g], nz)
        return pl.ds(pl.multiple_of((dp * ne + chip * 2) * CAP, 2 * CAP), 2 * CAP)

    def x_copy(kind, g, way):
        rows = group_rows(i, g)
        return remote(recv[kind].at[rows], recv[kind].at[rows], xs.at[kind, g, way], xr.at[kind, g, way],
                      (right, left)[way])

    def f_copy(kind, g):
        way = (g + kind) % 2
        rows = group_rows(mod(i - 1, nd) if way == 0 else mod(i + 1, nd), g)
        return remote(recv[kind].at[rows], recv[kind].at[rows], fs.at[kind, g], fr.at[kind, g], (right, left)[way])

    groups = len(Z_ORDER)

    def z_send(kind, g):
        for dc in (0, 1):
            if (Z_ORDER[g], dc) != (0, 0):
                z_copy(kind, Z_ORDER[g], dc).start()

    for kind in (0, 1):
        own(kind).start()
    for g in range(groups):
        z_send(0, g)
    steps = [(kind, g) for kind in (0, 1) for g in range(groups)]
    for t, (kind, g) in enumerate(steps):
        for dc in (0, 1):
            if (Z_ORDER[g], dc) == (0, 0):
                own(kind).wait()
            else:
                z_copy(kind, Z_ORDER[g], dc).wait_recv()
        for way in (0, 1):
            x_copy(kind, g, way).start()
        if kind == 0:
            z_send(1, g)
        if t:
            lk, lg = steps[t - 1]
            x_copy(lk, lg, (lg + lk) % 2).wait_recv()
            f_copy(lk, lg).start()
    lk, lg = steps[-1]
    x_copy(lk, lg, (lg + lk) % 2).wait_recv()
    f_copy(lk, lg).start()
    for kind, g in steps:
        x_copy(kind, g, 1 - (g + kind) % 2).wait_recv()
        f_copy(kind, g).wait_recv()
    for kind, g in steps:
        for dc in (0, 1):
            if (Z_ORDER[g], dc) != (0, 0):
                z_copy(kind, Z_ORDER[g], dc).wait_send()
        for way in (0, 1):
            x_copy(kind, g, way).wait_send()
        f_copy(kind, g).wait_send()


def dispatch(acts, grads, ids, weights, nd, ne):
    tokens, width = acts.shape
    rows = nd * ne * CAP
    slots = ne * CAP
    vmem, hbm = pl.BlockSpec(memory_space=pltpu.VMEM), pl.BlockSpec(memory_space=pltpu.HBM)
    dma = pltpu.SemaphoreType.DMA
    groups = len(Z_ORDER)
    wide = jax.ShapeDtypeStruct((rows, width), BF16)
    small = jax.ShapeDtypeStruct((slots, width), BF16)
    outs = pl.pallas_call(
        functools.partial(fwd_kernel, nd, ne),
        out_shape=(wide, wide, small, small, jax.ShapeDtypeStruct((slots, tokens), BF16)),
        in_specs=[vmem] * 4,
        out_specs=(hbm, hbm, hbm, hbm, vmem),
        scratch_shapes=[pltpu.VMEM((slots, width), BF16), pltpu.VMEM((slots, width), BF16),
                        dma((4,)), dma((2, ne)), dma((2, ne)), dma((2, groups, 2)), dma((2, groups, 2)),
                        dma((2, groups)), dma((2, groups))],
        compiler_params=pltpu.CompilerParams(collective_id=0, has_side_effects=True, vmem_limit_bytes=VMEM_LIMIT),
        name="dispatch",
    )(acts, grads, ids, weights)
    return outs[0], outs[1], outs[4]


def expert_kernel(rx_ref, rg_ref, wg_ref, wu_ref, wd_ref, part_ref, score_ref, dwg_ref, dwu_ref, dwd_ref,
                  delta, hid):
    rows, width = rx_ref.shape
    hs = wg_ref.shape[1]
    nt = (((1,), (1,)), ((), ()))
    tn = (((0,), (0,)), ((), ()))
    tall = 256

    def forward(k, _):
        r = pl.ds(pl.multiple_of(k * tall, tall), tall)
        xr, gr = rx_ref[r, :], rg_ref[r, :]
        gate = jnp.dot(xr, wg_ref[...], preferred_element_type=F32)
        up = jnp.dot(xr, wu_ref[...], preferred_element_type=F32)
        gh = lax.dot_general(gr, wd_ref[...], nt, preferred_element_type=F32)
        sig = jax.nn.sigmoid(gate)
        swish = gate * sig
        hidden = swish * up
        score = jnp.sum(hidden * gh, axis=1, keepdims=True)
        lane = lax.broadcasted_iota(jnp.int32, (tall, 128), 1)
        row = jnp.bitwise_and(lax.broadcasted_iota(jnp.int32, (tall, 128), 0), CAP - 1)
        spread = jnp.where(lane == row, jnp.broadcast_to(score, (tall, 128)), 0.0)
        blocks = tall // CAP
        score_ref[pl.ds(k * blocks, blocks)] = jnp.sum(spread.reshape(blocks, CAP, 128), axis=1, keepdims=True)
        hid[r, :] = hidden.astype(BF16)
        delta[r, 0:hs] = (gh * up * sig * (1.0 + gate * (1.0 - sig))).astype(BF16)
        delta[r, hs:] = (gh * swish).astype(BF16)
        return 0

    lax.fori_loop(0, rows // tall, forward, 0)
    wide = 256
    dl, hd = delta[...], hid[...]

    def backward(t, _):
        cols = pl.ds(pl.multiple_of(t * wide, wide), wide)
        part = lax.dot_general(dl[:, :hs], wg_ref[cols, :], nt, preferred_element_type=F32)
        part += lax.dot_general(dl[:, hs:], wu_ref[cols, :], nt, preferred_element_type=F32)
        part_ref[:, cols] = part.astype(BF16)
        both = lax.dot_general(rx_ref[:, cols], dl, tn, preferred_element_type=F32).astype(BF16)
        dwg_ref[cols, :] = both[:, :hs]
        dwu_ref[cols, :] = both[:, hs:]
        dwd_ref[:, cols] = lax.dot_general(hd, rg_ref[:, cols], tn, preferred_element_type=F32).astype(BF16)
        return 0

    lax.fori_loop(0, width // wide, backward, 0)


def experts(rx, rg, wg, wu, wd):
    rows, width = rx.shape
    hs = wg.shape[1]
    vmem = pl.BlockSpec(memory_space=pltpu.VMEM)
    return pl.pallas_call(
        expert_kernel,
        out_shape=(jax.ShapeDtypeStruct((rows, width), BF16), jax.ShapeDtypeStruct((rows // CAP, 1, 128), F32),
                   jax.ShapeDtypeStruct((width, hs), BF16), jax.ShapeDtypeStruct((width, hs), BF16),
                   jax.ShapeDtypeStruct((hs, width), BF16)),
        in_specs=[vmem] * 5,
        out_specs=(vmem,) * 5,
        scratch_shapes=[pltpu.VMEM((rows, 2 * hs), BF16), pltpu.VMEM((rows, hs), BF16)],
        compiler_params=pltpu.CompilerParams(vmem_limit_bytes=VMEM_LIMIT),
        name="experts",
    )(rx, rg, wg, wu, wd)


def ret_kernel(nd, ne, pieces, part, score, smap, ids_ref, w_ref, out_ref, gwg_ref, rows_hbm, fin_hbm,
               b1, b2, bu, fin, back, snext, sc3, own_score, slot_score,
               lsem, s1s, s1r, s2s, s2r, sus, sur, zs, zr, cs, cr, es, er, ms, mr):
    p, i, e = place()
    npipe = lax.axis_size("pipe")
    slots, tokens = smap.shape
    width = part.shape[1]
    right, left = (p, mod(i + 1, nd), e), (p, mod(i - 1, nd), e)
    prev, nxt = mod(p - 1, npipe), mod(p + 1, npipe)
    chosen = ids_ref.shape[0]

    barrier = pltpu.get_barrier_semaphore()

    def greet(device):
        pl.semaphore_signal(barrier, inc=1, device_id=device, device_id_type=MESH)

    for d in range(1, nd):
        greet((p, mod(i + d, nd), e))
    for d in range(1, ne):
        greet((p, i, lax.rem(e + d, ne)))
    for d in range(ne):
        greet((prev, i, lax.rem(e + d, ne)))
        greet((nxt, i, lax.rem(e + d, ne)))
    pl.semaphore_wait(barrier, nd - 1 + ne - 1 + 2 * ne)

    def chunk(dp):
        return pl.ds(pl.multiple_of(dp * slots, slots), slots)

    def one(dp):
        return mod(i + dp, nd)

    cols = [pl.ds(start, size) for start, size in pieces]
    sides = (right, left)

    def step1(q):
        return remote(part.at[chunk(one(2)), cols[q]], b1.at[:, cols[q]], s1s.at[q], s1r.at[q], sides[q % 2])

    def plain(q):
        src = one(-1) if q % 2 == 0 else one(1)
        return remote(part.at[chunk(src), cols[q]], bu.at[:, cols[q]], sus.at[q], sur.at[q], sides[1 - q % 2])

    def step2(q):
        return remote(b1.at[:, cols[q]], b2.at[:, cols[q]], s2s.at[q], s2r.at[q], sides[q % 2])

    def map_copy():
        return remote(smap, snext, ms.at[0], mr.at[0], (prev, i, e))

    def score_x(d):
        return remote(score.at[pl.ds(one(d) * ne, ne)], sc3.at[d - 1], cs.at[d - 1], cr.at[d - 1], (p, one(d), e))

    def score_z(d):
        target = lax.rem(e + d, ne)
        return remote(own_score.at[target], slot_score.at[e], es.at[d], er.at[d], (p, i, target))

    pairs = len(pieces) // 2
    pair_cols = [pl.ds(pieces[2 * q][0], pieces[2 * q][1] + pieces[2 * q + 1][1]) for q in range(pairs)]

    def z_copy(pair, d):
        target = lax.rem(e + d, ne)
        return remote(fin_hbm.at[eight(target * CAP), pair_cols[pair]], rows_hbm.at[eight(e * CAP), pair_cols[pair]],
                      zs.at[pair, d], zr.at[pair, d], (prev, i, target))

    for q in range(len(pieces)):
        step1(q).start()
        if q % 2:
            plain(q - 1).start()
            plain(q).start()
        if q == 1:
            map_copy().start()
            for d in range(1, nd):
                score_x(d).start()

    def finish(pair):
        for q in (2 * pair, 2 * pair + 1):
            plain(q).wait_recv()
            step2(q).wait_recv()
        here = pair_cols[pair]
        total = part[chunk(i), here].astype(F32) + b2[:, here].astype(F32) + bu[:, here].astype(F32)
        fin[:, here] = total.astype(BF16)
        copy = pltpu.make_async_copy(fin.at[:, here], fin_hbm.at[:, here], lsem.at[0])
        copy.start()
        copy.wait()
        for d in range(ne):
            z_copy(pair, d).start()

    for pair in range(pairs):
        for q in (2 * pair, 2 * pair + 1):
            step1(q).wait_recv()
            mine = one(1) if q % 2 == 0 else one(-1)
            total = part[chunk(mine), cols[q]].astype(F32) + b1[:, cols[q]].astype(F32)
            b1[:, cols[q]] = total.astype(BF16)
            step2(q).start()
        if pair:
            finish(pair - 1)
        else:
            for d in range(1, nd):
                score_x(d).wait_recv()
            own_score[...] = score[pl.ds(i * ne, ne)] + sc3[0] + sc3[1] + sc3[2]
            slot_score[e] = own_score[e]
            for d in range(1, ne):
                score_z(d).start()
    finish(pairs - 1)

    for d in range(1, ne):
        score_z(d).wait_recv()
    column = jnp.broadcast_to(slot_score[...], (ne, CAP, 128)).reshape(slots, 128)
    expert, rank = slot_maps(ids_ref, slots, tokens)
    lane = lax.broadcasted_iota(jnp.int32, (slots, 128), 1)
    column = jnp.sum(jnp.where(lane == jnp.bitwise_and(lax.broadcasted_iota(jnp.int32, (slots, 128), 0), CAP - 1),
                               column, 0.0), axis=1, keepdims=True)
    spread = smap[...].astype(F32) * column
    for k in range(chosen):
        picked = jnp.sum(jnp.where(ids_ref[k] == expert, spread, 0.0), axis=0, keepdims=True)
        gwg_ref[k] = picked / w_ref[k]
    map_copy().wait_recv()
    tn = (((0,), (0,)), ((), ()))
    for pair in range(pairs):
        for d in range(ne):
            z_copy(pair, d).wait_recv()
        here = pair_cols[pair]
        copy = pltpu.make_async_copy(rows_hbm.at[:, here], back.at[:, here], lsem.at[1])
        copy.start()
        copy.wait()
        out_ref[:, here] = lax.dot_general(snext[...], back[:, here], tn, preferred_element_type=F32).astype(BF16)
    for q in range(len(pieces)):
        step1(q).wait_send()
        plain(q).wait_send()
        step2(q).wait_send()
    map_copy().wait_send()
    for d in range(1, nd):
        score_x(d).wait_send()
    for d in range(1, ne):
        score_z(d).wait_send()
    for pair in range(pairs):
        for d in range(ne):
            z_copy(pair, d).wait_send()


def combine(part, score, smap, ids, weights, nd, ne):
    slots, tokens = smap.shape
    width = part.shape[1]
    pieces = [(start, 512) for start in range(0, width, 512)]
    vmem, hbm = pl.BlockSpec(memory_space=pltpu.VMEM), pl.BlockSpec(memory_space=pltpu.HBM)
    dma = pltpu.SemaphoreType.DMA
    block = pltpu.VMEM((slots, width), BF16)
    small = jax.ShapeDtypeStruct((slots, width), BF16)
    n = len(pieces)
    outs = pl.pallas_call(
        functools.partial(ret_kernel, nd, ne, pieces),
        out_shape=(jax.ShapeDtypeStruct((tokens, width), BF16), jax.ShapeDtypeStruct(ids.shape, F32), small, small),
        in_specs=[vmem] * 5,
        out_specs=(vmem, vmem, hbm, hbm),
        scratch_shapes=[block] * 5 + [
            pltpu.VMEM((slots, tokens), BF16), pltpu.VMEM((nd - 1, ne, 1, 128), F32), pltpu.VMEM((ne, 1, 128), F32),
            pltpu.VMEM((ne, 1, 128), F32), dma((2,))] + [dma((n,))] * 6 + [dma((n // 2, ne))] * 2
            + [dma((nd - 1,))] * 2 + [dma((ne,))] * 2 + [dma((1,))] * 2,
        compiler_params=pltpu.CompilerParams(collective_id=1, has_side_effects=True, vmem_limit_bytes=VMEM_LIMIT),
        name="combine",
    )(part, score, smap, ids, weights)
    return outs[0], outs[1]


def shards(block_input, output_grad, expert_ids, gate_weights, gate_proj, up_proj, down_proj):
    nd, ne = lax.axis_size("dp"), lax.axis_size("expert")
    ids = jnp.transpose(expert_ids, (2, 0, 1))
    weights = jnp.transpose(gate_weights, (2, 0, 1))
    rx, rg, smap = dispatch(block_input[0], output_grad[0], ids, weights, nd, ne)
    part, score, dwg, dwu, dwd = experts(rx, rg, gate_proj[0, 0], up_proj[0, 0], down_proj[0, 0])
    received, gwg = combine(part, score, smap, ids, weights, nd, ne)
    return (received[None], jnp.transpose(gwg, (1, 2, 0)), dwg[None, None], dwu[None, None], dwd[None, None])


def solution(mesh):
    in_specs = (
        P("pipe", ("dp", "expert"), None),
        P("pipe", ("dp", "expert"), None),
        P("pipe", ("dp", "expert"), None),
        P("pipe", ("dp", "expert"), None),
        P("pipe", "expert", None, "dp"),
        P("pipe", "expert", None, "dp"),
        P("pipe", "expert", "dp", None),
    )
    out_specs = (
        P("pipe", ("dp", "expert"), None),
        P("pipe", ("dp", "expert"), None),
        P("pipe", "expert", None, "dp"),
        P("pipe", "expert", None, "dp"),
        P("pipe", "expert", "dp", None),
    )
    return jax.shard_map(shards, mesh=mesh, in_specs=in_specs, out_specs=out_specs, check_vma=False)
```

time: 389 us -> 147 us (0.38)
  waiting for transfers between devices: 273 us -> 0 us
  Pallas kernels: 0 us -> 144 us
  local copies, waits for them, and re-layouts: 45.5 us -> 2.65 us
  starting transfers between devices: 34.5 us -> 0 us
  matrix products: 26.4 us -> 0 us
  other arithmetic: 6.77 us -> 0 us
    all_to_all x4 -> x0, waiting for transfers between devices: 272 us -> none  [the longest x1 135 us: shards(): lax.all_to_all(partial_value, ('dp', 'expert'), split_axis=1, concat_axis...]
    pallas_call x0 -> x3, Pallas kernels: none -> 144 us  [the longest x1 68.9 us: dispatch(): pl.pallas_call(functools.partial(fwd_kernel, nd, ne), out_shape=(wide, wi...]
    all_to_all x4 -> x0, starting transfers between devices: 31.7 us -> none  [the longest x1 13.3 us: shards(): lax.all_to_all(acts_copies, ('dp', 'expert'), split_axis=0, concat_axis=1...]
    dot_general x9 -> x0, matrix products: 26.4 us -> none  [the longest x1 4.38 us: shards(): jnp.einsum('erh,erd->ehd', hidden.astype(jnp.bfloat16), recv_grad, prefer...]
    add x1 -> x0, local copies, waits for them, and re-layouts: 19.1 us -> none  [shards(): jnp.einsum('erh,edh->erd', delta_gate, gate_local, preferred_element_type...]
    gather x5 -> x0, local copies, waits for them, and re-layouts: 10.2 us -> none  [the longest x2 5.11 us: shards(): padded_scores[slot_index] / route_weight.reshape(-1)]
    unnamed x19 -> x4, local copies, waits for them, and re-layouts: 9.41 us -> 2.65 us
    broadcast_in_dim x3 -> x0, local copies, waits for them, and re-layouts: 4.24 us -> none  [the longest x1 2.1 us: shards(): jnp.broadcast_to(send_grad[None], (dp_count,) + send_grad.shape)]
  transfers between devices with their start and end apart: 5 -> 0, of which waited for: 4 -> 0; matrix products, arithmetic and copies ran while one was open for 11% -> 0% of each run, Pallas kernels for 0% -> 0%
where the time goes in v1:
time: 147 us
  Pallas kernels  144 us (98%)
  local copies, waits for them, and re-layouts  2.65 us (2%)
    pallas_call x1, Pallas kernels, dispatch(): pl.pallas_call(functools.partial(fwd_kernel, nd, ne), out_shape=(wide, wi...  68.9 us
    pallas_call x1, Pallas kernels, combine(): pl.pallas_call(functools.partial(ret_kernel, nd, ne, pieces), out_shape=(...  57.9 us
    pallas_call x1, Pallas kernels, experts(): pl.pallas_call(expert_kernel, out_shape=(jax.ShapeDtypeStruct((rows, widt...  16.9 us

profile of v1, /device:TPU:1, one launch (start us, length us, event | category | flops | bytes accessed | tf_op | source)
XLA Modules:
  0.0 147.0 jit_solution(12129889970402271893)
XLA Ops:
  0.6 68.9 %dispatch.1 = (bf16[512,3072]{1,0:T(8,128)(2,1)}, bf16[512,3072]{1,0:T(8,128)(2,1)}, bf16[128,3072]{1,0:T(8,128)(2,1)}, bf16[128,3072]{1,0:T(8,128)(2,1)}, bf16[128,128]{1,0:T(8,128)(2,1)}) custom-call(bf16[128,3072]{1,0:T(8,128)(2,1)} %bitcast.15, bf16[128,3072]{1,0:T(8,128)(2,1)} %bitcast.16, s32[6,1,128]{2,1,0:T(1,128)} %bitcast.18, f32[6,1,128]{2,1,0:T(1,128)} %bitcast.20), custom_call_target="tpu_custom_call" | custom-call | tf_op jit(solution)/shard_map/dispatch/pallas_call | solution.py:156
  69.5 16.9 %experts.1 = (bf16[512,3072]{1,0:T(8,128)(2,1)}, f32[64,1,128]{2,1,0:T(1,128)}, bf16[3072,256]{1,0:T(8,128)(2,1)}, bf16[3072,256]{1,0:T(8,128)(2,1)}, bf16[256,3072]{1,0:T(8,128)(2,1)}) custom-call(bf16[512,3072]{1,0:T(8,128)(2,1)} %get-tuple-element.15.rx_ref, bf16[512,3072]{1,0:T(8,128)(2,1)} %get-tuple-element.16.rg_ref, bf16[3072,256]{1,0:T(8,128)(2,1)} %bitcast.12, ...), custom_call_target="tpu_custom_call" | custom-call | tf_op jit(solution)/shard_map/experts/pallas_call | solution.py:220
  86.4 57.9 %combine.1 = (bf16[128,3072]{1,0:T(8,128)(2,1)}, f32[6,1,128]{2,1,0:T(1,128)}, bf16[128,3072]{1,0:T(8,128)(2,1)}, bf16[128,3072]{1,0:T(8,128)(2,1)}) custom-call(bf16[512,3072]{1,0:T(8,128)(2,1)} %get-tuple-element.17.part, f32[64,1,128]{2,1,0:T(1,128)} %get-tuple-element.18.score, bf16[128,128]{1,0:T(8,128)(2,1)} %get-tuple-element.19.smap, ...), custom_call_target="tpu_custom_call" | custom-call | tf_op jit(solution)/shard_map/combine/pallas_call | solution.py:380
  144.3 0.0 copy-start
  144.3 2.1 %copy.14 = bf16[1,128,3072]{2,1,0:T(8,128)(2,1)} copy(bf16[1,128,3072]{2,1,0:T(8,128)(2,1)} %bitcast.17) | data formatting | bytes 1572864
  146.4 0.0 copy-done
  146.4 0.6 copy.15
Async XLA Ops:
  144.3 2.1 %copy-start = (f32[6,1,128]{2,1,0:T(1,128)S(1)}, f32[6,1,128]{2,1,0:T(1,128)}, u32[]{:S(2)}) copy-start(f32[6,1,128]{2,1,0:T(1,128)} %get-tuple-element.21) | copy-start | bytes 9220

commit v2 on v0

v2 whole, which is shorter than its diff:
```python
import functools
import jax
import jax.numpy as jnp
from jax import lax
from jax.experimental import pallas as pl
from jax.experimental.pallas import tpu as pltpu
from jax.sharding import PartitionSpec as P

MESH = pl.DeviceIdType.MESH
CAP = 8
F32 = jnp.float32
BF16 = jnp.bfloat16
VMEM_LIMIT = 58 << 20
Z_ORDER = (0, 1, -1, 2, -2, 3, -3, 4)


def mod(value, count):
    return lax.rem(value + count, count)


def place():
    return lax.axis_index("pipe"), lax.axis_index("dp"), lax.axis_index("expert")


def remote(src, dst, send_sem, recv_sem, device):
    return pltpu.make_async_remote_copy(
        src_ref=src, dst_ref=dst, send_sem=send_sem, recv_sem=recv_sem,
        device_id=device, device_id_type=MESH)


def eight(row):
    return pl.ds(pl.multiple_of(row, 8), 8)


def slot_maps(ids_ref, slots, tokens):
    slot = lax.broadcasted_iota(jnp.int32, (slots, tokens), 0)
    expert = lax.shift_right_logical(slot, 3)
    rank = jnp.bitwise_and(slot, 7)
    return expert, rank


def routed_kernel(nd, ne, pieces, x_ref, dy_ref, ids_ref, w_ref, wg_hbm, wu_hbm, wd_hbm,
                  rows_hbm, next_hbm, score_hbm, smap_ref, rx_hbm, rg_hbm, delta_hbm, hidden_hbm,
                  sx, sg, rx, rg, wg, wu, wd, gu, delta, hid, part, b1, b2, bu, fin, score, sc3, own_score,
                  lsem, zs, zr, xs, xr, fs, fr, s1s, s1r, s2s, s2r, sus, sur, ys, yr, cs, cr, es, er, ms, mr):
    p, i, e = place()
    z, c = e // 2, e % 2
    nz = ne // 2
    npipe = lax.axis_size("pipe")
    tokens, width = x_ref.shape
    slots = ne * CAP
    chosen = ids_ref.shape[0]
    hs = wg.shape[1]
    groups = len(Z_ORDER)
    nt = (((1,), (1,)), ((), ()))
    right, left = (p, mod(i + 1, nd), e), (p, mod(i - 1, nd), e)
    sides = (right, left)
    prev, nxt = mod(p - 1, npipe), mod(p + 1, npipe)

    barrier = pltpu.get_barrier_semaphore()

    def greet(device):
        pl.semaphore_signal(barrier, inc=1, device_id=device, device_id_type=MESH)

    for d in range(1, nd):
        greet((p, mod(i + d, nd), e))
    for d in range(1, ne):
        greet((p, i, lax.rem(e + d, ne)))
    for d in range(ne):
        greet((prev, i, lax.rem(e + d, ne)))
        greet((nxt, i, lax.rem(e + d, ne)))

    loads = [pltpu.make_async_copy(a, b, lsem.at[n]) for n, (a, b) in enumerate(
        ((wg_hbm, wg), (wu_hbm, wu), (wd_hbm, wd)))]
    for copy in loads:
        copy.start()

    expert, rank_of = slot_maps(ids_ref, slots, tokens)
    hit = jnp.zeros((slots, tokens), F32)
    weight = jnp.zeros((slots, tokens), F32)
    for k in range(chosen):
        same = ids_ref[k] == expert
        hit = jnp.where(same, 1.0, hit)
        weight = jnp.where(same, w_ref[k], weight)
    before = (lax.broadcasted_iota(jnp.int32, (tokens, tokens), 0)
              < lax.broadcasted_iota(jnp.int32, (tokens, tokens), 1))
    rank = jnp.dot(hit.astype(BF16), jnp.where(before, 1.0, 0.0).astype(BF16), preferred_element_type=F32)
    table = jnp.where(rank == rank_of.astype(F32), hit, 0.0)
    slot_weight = jnp.sum(table * weight, axis=1, keepdims=True)
    table = table.astype(BF16)
    smap_ref[...] = table
    sx[...] = jnp.dot(table, x_ref[...], preferred_element_type=F32).astype(BF16)
    pl.semaphore_wait(barrier, nd - 1 + ne - 1 + 2 * ne)

    send, recv = (sx, sg), (rx, rg)

    def z_copy(kind, dz, dc):
        n = (dz % nz) * 2 + dc
        target = mod(z + dz, nz) * 2 + (c + dc - 2 * c * dc)
        return remote(send[kind].at[eight(target * CAP)], recv[kind].at[eight((i * ne + e) * CAP)],
                      zs.at[kind, n], zr.at[kind, n], (p, i, target))

    def own(kind):
        return pltpu.make_async_copy(send[kind].at[eight(e * CAP)], recv[kind].at[eight((i * ne + e) * CAP)],
                                     lsem.at[3 + kind])

    def group_rows(dp, g):
        chip = mod(z - Z_ORDER[g], nz)
        return pl.ds(pl.multiple_of((dp * ne + chip * 2) * CAP, 2 * CAP), 2 * CAP)

    def x_copy(kind, g, way):
        rows = group_rows(i, g)
        return remote(recv[kind].at[rows], recv[kind].at[rows], xs.at[kind, g, way], xr.at[kind, g, way], sides[way])

    def f_way(kind, g):
        return (g + kind) % 2

    def f_copy(kind, g):
        way = f_way(kind, g)
        rows = group_rows(mod(i - 1, nd) if way == 0 else mod(i + 1, nd), g)
        return remote(recv[kind].at[rows], recv[kind].at[rows], fs.at[kind, g], fr.at[kind, g], sides[way])

    def z_send(kind, g):
        for dc in (0, 1):
            if (Z_ORDER[g], dc) != (0, 0):
                z_copy(kind, Z_ORDER[g], dc).start()

    def z_step(kind, g):
        for dc in (0, 1):
            if (Z_ORDER[g], dc) == (0, 0):
                own(kind).wait()
            else:
                z_copy(kind, Z_ORDER[g], dc).wait_recv()
        for way in (0, 1):
            x_copy(kind, g, way).start()

    def forward(kind, g):
        x_copy(kind, g, f_way(kind, g)).wait_recv()
        f_copy(kind, g).start()

    def map_copy():
        return remote(smap_ref, next_hbm, ms.at[0], mr.at[0], (prev, i, e))

    own(0).start()
    for g in range(groups):
        z_send(0, g)
    sg[...] = (slot_weight * jnp.dot(table, dy_ref[...], preferred_element_type=F32)).astype(BF16)
    own(1).start()
    map_copy().start()

    def one(dp):
        return mod(i + dp, nd)

    def chunk(dp):
        return pl.ds(pl.multiple_of(dp * slots, slots), slots)

    def inner(dp):
        r = chunk(one(dp))
        gu[r, 0:hs] = jnp.dot(rx[r, :], wg[...], preferred_element_type=F32)
        gu[r, hs:] = jnp.dot(rx[r, :], wu[...], preferred_element_type=F32)

    def act(dp):
        r = chunk(one(dp))
        gate, up = gu[r, 0:hs], gu[r, hs:]
        gh = lax.dot_general(rg[r, :], wd[...], nt, preferred_element_type=F32)
        sig = jax.nn.sigmoid(gate)
        swish = gate * sig
        hidden = swish * up
        total = jnp.sum(hidden * gh, axis=1, keepdims=True)
        lane = lax.broadcasted_iota(jnp.int32, (slots, 128), 1)
        row = jnp.bitwise_and(lax.broadcasted_iota(jnp.int32, (slots, 128), 0), CAP - 1)
        spread = jnp.where(lane == row, jnp.broadcast_to(total, (slots, 128)), 0.0)
        score[pl.ds(one(dp) * ne, ne)] = jnp.sum(spread.reshape(ne, CAP, 128), axis=1, keepdims=True)
        hid[r, :] = hidden.astype(BF16)
        delta[r, 0:hs] = (gh * up * sig * (1.0 + gate * (1.0 - sig))).astype(BF16)
        delta[r, hs:] = (gh * swish).astype(BF16)

    def partial(dp):
        r = chunk(one(dp))
        dg, du = delta[r, 0:hs], delta[r, hs:]
        wide = 512
        for t in range(width // wide):
            cut = slice(t * wide, (t + 1) * wide)
            value = lax.dot_general(dg, wg[cut, :], nt, preferred_element_type=F32)
            value += lax.dot_general(du, wu[cut, :], nt, preferred_element_type=F32)
            part[r, cut] = value.astype(BF16)

    for g in range(groups):
        z_step(0, g)
        z_send(1, g)
        if g:
            forward(0, g - 1)
    for copy in loads:
        copy.wait()
    order = (0, -1, 1, 2)
    for g in range(groups):
        z_step(1, g)
        forward(*((1, g - 1) if g else (0, groups - 1)))
        if 3 <= g < 7:
            if g == 4:
                for h in range(groups):
                    x_copy(0, h, 1 - f_way(0, h)).wait_recv()
            if g == 6:
                for h in range(groups):
                    f_copy(0, h).wait_recv()
            inner(order[g - 3])
    act(0)
    forward(1, groups - 1)
    for g in range(groups):
        x_copy(1, g, 1 - f_way(1, g)).wait_recv()

    cols = [pl.ds(start, size) for start, size in pieces]

    def step1(q):
        return remote(part.at[chunk(one(2)), cols[q]], b1.at[:, cols[q]], s1s.at[q], s1r.at[q], sides[q % 2])

    def plain(q):
        src = one(-1) if q % 2 == 0 else one(1)
        return remote(part.at[chunk(src), cols[q]], bu.at[:, cols[q]], sus.at[q], sur.at[q], sides[1 - q % 2])

    def step2(q):
        return remote(b1.at[:, cols[q]], b2.at[:, cols[q]], s2s.at[q], s2r.at[q], sides[q % 2])

    def score_x(d):
        return remote(score.at[pl.ds(one(d) * ne, ne)], sc3.at[d - 1], cs.at[d - 1], cr.at[d - 1], (p, one(d), e))

    def score_z(d):
        target = lax.rem(e + d, ne)
        return remote(own_score.at[target], score_hbm.at[e], es.at[d], er.at[d], (p, i, target))

    def score_own():
        return pltpu.make_async_copy(own_score.at[e], score_hbm.at[e], lsem.at[5])

    pairs = len(pieces) // 2
    pair_cols = [pl.ds(pieces[2 * q][0], pieces[2 * q][1] + pieces[2 * q + 1][1]) for q in range(pairs)]

    def y_copy(pair, d):
        target = lax.rem(e + d, ne)
        return remote(fin.at[eight(target * CAP), pair_cols[pair]], rows_hbm.at[eight(e * CAP), pair_cols[pair]],
                      ys.at[pair, d], yr.at[pair, d], (prev, i, target))

    def both(copy, pair):
        for q in (2 * pair, 2 * pair + 1):
            copy(q).start()

    def middle(pair):
        for q in (2 * pair, 2 * pair + 1):
            step1(q).wait_recv()
            mine = one(1) if q % 2 == 0 else one(-1)
            total = part[chunk(mine), cols[q]].astype(F32) + b1[:, cols[q]].astype(F32)
            b1[:, cols[q]] = total.astype(BF16)
            step2(q).start()

    def finish(pair):
        for q in (2 * pair, 2 * pair + 1):
            plain(q).wait_recv()
            step2(q).wait_recv()
        here = pair_cols[pair]
        total = part[chunk(i), here].astype(F32) + b2[:, here].astype(F32) + bu[:, here].astype(F32)
        fin[:, here] = total.astype(BF16)
        for d in range(ne):
            y_copy(pair, d).start()

    act(-1)
    act(1)
    partial(-1)
    partial(1)
    both(plain, 0)
    both(plain, 1)
    for g in range(groups):
        f_copy(1, g).wait_recv()
    act(2)
    partial(2)
    both(step1, 0)
    both(step1, 1)
    for d in range(1, nd):
        score_x(d).start()
    saves = [pltpu.make_async_copy(a, b, lsem.at[6 + n]) for n, (a, b) in enumerate(
        ((rx, rx_hbm), (rg, rg_hbm), (delta, delta_hbm), (hid, hidden_hbm)))]
    for copy in saves:
        copy.start()
    partial(0)
    middle(0)
    both(plain, 2)
    both(step1, 2)
    middle(1)
    finish(0)
    for d in range(1, nd):
        score_x(d).wait_recv()
    own_score[...] = score[pl.ds(i * ne, ne)] + sc3[0] + sc3[1] + sc3[2]
    score_own().start()
    for d in range(1, ne):
        score_z(d).start()
    middle(2)
    finish(1)
    finish(2)

    for copy in saves:
        copy.wait()
    for kind in (0, 1):
        for g in range(groups):
            for dc in (0, 1):
                if (Z_ORDER[g], dc) != (0, 0):
                    z_copy(kind, Z_ORDER[g], dc).wait_send()
            for way in (0, 1):
                x_copy(kind, g, way).wait_send()
            f_copy(kind, g).wait_send()
    for q in range(len(pieces)):
        step1(q).wait_send()
        plain(q).wait_send()
        step2(q).wait_send()
    map_copy().wait_send()
    map_copy().wait_recv()
    score_own().wait()
    for d in range(1, nd):
        score_x(d).wait_send()
    for d in range(1, ne):
        score_z(d).wait_send()
        score_z(d).wait_recv()
    for pair in range(pairs):
        for d in range(ne):
            y_copy(pair, d).wait_send()
            y_copy(pair, d).wait_recv()


def routed(acts, grads, ids, weights, wg, wu, wd, nd, ne):
    tokens, width = acts.shape
    hs = wg.shape[1]
    slots = ne * CAP
    rows = nd * slots
    edges = ((0, 640), (1280, 512), (2304, 384))
    pieces = [(start + half * size, size) for start, size in edges for half in (0, 1)]
    vmem, hbm = pl.BlockSpec(memory_space=pltpu.VMEM), pl.BlockSpec(memory_space=pltpu.HBM)
    dma = pltpu.SemaphoreType.DMA
    groups, n = len(Z_ORDER), len(pieces)
    shape = jax.ShapeDtypeStruct
    block = pltpu.VMEM((slots, width), BF16)
    full = pltpu.VMEM((rows, width), BF16)
    return pl.pallas_call(
        functools.partial(routed_kernel, nd, ne, pieces),
        out_shape=(shape((slots, width), BF16), shape((slots, tokens), BF16), shape((ne, 1, 128), F32),
                   shape((slots, tokens), BF16), shape((rows, width), BF16), shape((rows, width), BF16),
                   shape((rows, 2 * hs), BF16), shape((rows, hs), BF16)),
        in_specs=[vmem] * 4 + [hbm] * 3,
        out_specs=(hbm, hbm, hbm, vmem, hbm, hbm, hbm, hbm),
        scratch_shapes=[block, block, full, full, pltpu.VMEM(wg.shape, BF16), pltpu.VMEM(wu.shape, BF16),
                        pltpu.VMEM(wd.shape, BF16), pltpu.VMEM((rows, 2 * hs), F32), pltpu.VMEM((rows, 2 * hs), BF16),
                        pltpu.VMEM((rows, hs), BF16), full, block, block, block, block,
                        pltpu.VMEM((nd * ne, 1, 128), F32), pltpu.VMEM((nd - 1, ne, 1, 128), F32),
                        pltpu.VMEM((ne, 1, 128), F32),
                        dma((10,)), dma((2, ne)), dma((2, ne)), dma((2, groups, 2)), dma((2, groups, 2)),
                        dma((2, groups)), dma((2, groups))] + [dma((n,))] * 6 + [dma((n // 2, ne))] * 2
        + [dma((nd - 1,))] * 2 + [dma((ne,))] * 2 + [dma((1,))] * 2,
        compiler_params=pltpu.CompilerParams(collective_id=0, has_side_effects=True, vmem_limit_bytes=VMEM_LIMIT),
        name="routed",
    )(acts, grads, ids, weights, wg, wu, wd)


def local_kernel(rx, rg, delta, hid, rows, snext, smap, score, ids_ref, w_ref, out, gwg, dwg, dwu, dwd):
    tn = (((0,), (0,)), ((), ()))
    hs = hid.shape[1]
    slots, tokens = smap.shape

    @pl.when(pl.program_id(0) == 0)
    def _():
        ne = slots // CAP
        column = jnp.broadcast_to(score[...], (ne, CAP, 128)).reshape(slots, 128)
        expert, _ = slot_maps(ids_ref, slots, tokens)
        lane = lax.broadcasted_iota(jnp.int32, (slots, 128), 1)
        row = jnp.bitwise_and(lax.broadcasted_iota(jnp.int32, (slots, 128), 0), CAP - 1)
        column = jnp.sum(jnp.where(lane == row, column, 0.0), axis=1, keepdims=True)
        spread = smap[...].astype(F32) * column
        for k in range(ids_ref.shape[0]):
            picked = jnp.sum(jnp.where(ids_ref[k] == expert, spread, 0.0), axis=0, keepdims=True)
            gwg[k] = picked / w_ref[k]

    out[...] = lax.dot_general(snext[...], rows[...], tn, preferred_element_type=F32).astype(BF16)
    both = lax.dot_general(rx[...], delta[...], tn, preferred_element_type=F32).astype(BF16)
    dwg[...] = both[:, :hs]
    dwu[...] = both[:, hs:]
    dwd[...] = lax.dot_general(hid[...], rg[...], tn, preferred_element_type=F32).astype(BF16)


def local(rows, snext, score, smap, rx, rg, delta, hid, ids, weights):
    count, width = rx.shape
    hs = hid.shape[1]
    slots, tokens = smap.shape
    wide = 512

    def whole(array):
        return pl.BlockSpec(array.shape, lambda t: (0,) * array.ndim)

    def across(height):
        return pl.BlockSpec((height, wide), lambda t: (0, t))

    down = pl.BlockSpec((wide, hs), lambda t: (t, 0))
    shape = jax.ShapeDtypeStruct
    return pl.pallas_call(
        local_kernel,
        grid=(width // wide,),
        out_shape=(shape((tokens, width), BF16), shape(ids.shape, F32), shape((width, hs), BF16),
                   shape((width, hs), BF16), shape((hs, width), BF16)),
        in_specs=[across(count), across(count), whole(delta), whole(hid), across(slots), whole(snext), whole(smap),
                  whole(score), whole(ids), whole(weights)],
        out_specs=(across(tokens), whole(ids), down, down, across(hs)),
        compiler_params=pltpu.CompilerParams(vmem_limit_bytes=VMEM_LIMIT),
        name="local",
    )(rx, rg, delta, hid, rows, snext, smap, score, ids, weights)


def shards(block_input, output_grad, expert_ids, gate_weights, gate_proj, up_proj, down_proj):
    nd, ne = lax.axis_size("dp"), lax.axis_size("expert")
    ids = jnp.transpose(expert_ids, (2, 0, 1))
    weights = jnp.transpose(gate_weights, (2, 0, 1))
    outs = routed(block_input[0], output_grad[0], ids, weights, gate_proj[0, 0], up_proj[0, 0], down_proj[0, 0],
                  nd, ne)
    received, gwg, dwg, dwu, dwd = local(*outs, ids, weights)
    return (received[None], jnp.transpose(gwg, (1, 2, 0)), dwg[None, None], dwu[None, None], dwd[None, None])


def solution(mesh):
    in_specs = (
        P("pipe", ("dp", "expert"), None),
        P("pipe", ("dp", "expert"), None),
        P("pipe", ("dp", "expert"), None),
        P("pipe", ("dp", "expert"), None),
        P("pipe", "expert", None, "dp"),
        P("pipe", "expert", None, "dp"),
        P("pipe", "expert", "dp", None),
    )
    out_specs = (
        P("pipe", ("dp", "expert"), None),
        P("pipe", ("dp", "expert"), None),
        P("pipe", "expert", None, "dp"),
        P("pipe", "expert", None, "dp"),
        P("pipe", "expert", "dp", None),
    )
    return jax.shard_map(shards, mesh=mesh, in_specs=in_specs, out_specs=out_specs, check_vma=False)
```

time: 389 us -> 123 us (0.32)
  waiting for transfers between devices: 273 us -> 0 us
  Pallas kernels: 0 us -> 122 us
  local copies, waits for them, and re-layouts: 45.5 us -> 0 us
  starting transfers between devices: 34.5 us -> 0 us
  matrix products: 26.4 us -> 0 us
  other arithmetic: 6.77 us -> 0 us
    all_to_all x4 -> x0, waiting for transfers between devices: 272 us -> none  [the longest x1 135 us: shards(): lax.all_to_all(partial_value, ('dp', 'expert'), split_axis=1, concat_axis...]
    pallas_call x0 -> x2, Pallas kernels: none -> 122 us  [the longest x1 114 us: routed(): pl.pallas_call(functools.partial(routed_kernel, nd, ne, pieces), out_shap...]
    all_to_all x4 -> x0, starting transfers between devices: 31.7 us -> none  [the longest x1 13.3 us: shards(): lax.all_to_all(acts_copies, ('dp', 'expert'), split_axis=0, concat_axis=1...]
    dot_general x9 -> x0, matrix products: 26.4 us -> none  [the longest x1 4.38 us: shards(): jnp.einsum('erh,erd->ehd', hidden.astype(jnp.bfloat16), recv_grad, prefer...]
    add x1 -> x0, local copies, waits for them, and re-layouts: 19.1 us -> none  [shards(): jnp.einsum('erh,edh->erd', delta_gate, gate_local, preferred_element_type...]
    gather x5 -> x0, local copies, waits for them, and re-layouts: 10.2 us -> none  [the longest x2 5.11 us: shards(): padded_scores[slot_index] / route_weight.reshape(-1)]
    unnamed x19 -> x0, local copies, waits for them, and re-layouts: 9.41 us -> none
    broadcast_in_dim x3 -> x0, local copies, waits for them, and re-layouts: 4.24 us -> none  [the longest x1 2.1 us: shards(): jnp.broadcast_to(send_grad[None], (dp_count,) + send_grad.shape)]
  transfers between devices with their start and end apart: 5 -> 0, of which waited for: 4 -> 0; matrix products, arithmetic and copies ran while one was open for 11% -> 0% of each run, Pallas kernels for 0% -> 0%
where the time goes in v2:
time: 123 us
  Pallas kernels  122 us (99%)
    pallas_call x1, Pallas kernels, routed(): pl.pallas_call(functools.partial(routed_kernel, nd, ne, pieces), out_shap...  114 us
    pallas_call x1, Pallas kernels, local(): pl.pallas_call(local_kernel, grid=(width // wide,), out_shape=(shape((tok...  8.15 us

profile of v2, /device:TPU:1, one launch (start us, length us, event | category | flops | bytes accessed | tf_op | source)
XLA Modules:
  0.0 122.9 jit_solution(18419313594254955981)
XLA Ops:
  0.6 114.1 %routed.1 = (bf16[128,3072]{1,0:T(8,128)(2,1)}, bf16[128,128]{1,0:T(8,128)(2,1)}, f32[16,1,128]{2,1,0:T(1,128)}, bf16[128,128]{1,0:T(8,128)(2,1)}, bf16[512,3072...) custom-call(bf16[128,3072]{1,0:T(8,128)(2,1)} %bitcast.15, ...), custom_call_target="tpu_custom_call" | custom-call | tf_op jit(solution)/shard_map/routed/pallas_call | solution.py:339
  114.7 8.2 %local.1 = (bf16[128,3072]{1,0:T(8,128)(2,1)}, f32[6,1,128]{2,1,0:T(1,128)}, bf16[3072,256]{1,0:T(8,128)(2,1)}, bf16[3072,256]{1,0:T(8,128)(2,1)}, bf16[256,3072]{1,0:T(8,128)(2,1)}) custom-call(bf16[512,3072]{1,0:T(8,128)(2,1)} %get-tuple-element.18.rx, bf16[512,3072]{1,0:T(8,128)(2,1)} %get-tuple-element.19.rg, bf16[512,512]{1,0:T(8,128)(2,1)} %get-tuple-element.20.delta, ...), custom_call_target="tpu_custom_call" | custom-call | tf_op jit(solution)/shard_map/local/pallas_call | solution.py:398

commit v3 on v2

v3 whole, which is shorter than its diff:
```python
import functools
import jax
import jax.numpy as jnp
from jax import lax
from jax.experimental import pallas as pl
from jax.experimental.pallas import tpu as pltpu
from jax.sharding import PartitionSpec as P

MESH = pl.DeviceIdType.MESH
CAP = 8
F32 = jnp.float32
BF16 = jnp.bfloat16
VMEM_LIMIT = 58 << 20
Z_PLACES = (0, 1, -1, 2, -2, 3, -3, 4)
LOOK = 2
LAG = 4
PAIRS = ((1536, 1536), (1280, 1024, 768))


def mod(value, count):
    return lax.rem(value + count, count)


def place():
    return lax.axis_index("pipe"), lax.axis_index("dp"), lax.axis_index("expert")


def remote(src, dst, send_sem, recv_sem, device):
    return pltpu.make_async_remote_copy(
        src_ref=src, dst_ref=dst, send_sem=send_sem, recv_sem=recv_sem,
        device_id=device, device_id_type=MESH)


def eight(row):
    return pl.ds(pl.multiple_of(row, 8), 8)


def slot_maps(ids_ref, slots, tokens):
    slot = lax.broadcasted_iota(jnp.int32, (slots, tokens), 0)
    expert = lax.shift_right_logical(slot, 3)
    rank = jnp.bitwise_and(slot, 7)
    return expert, rank


def routed_kernel(nd, ne, pieces, x_hbm, dy_hbm, ids_hbm, w_hbm, wg_hbm, wu_hbm, wd_hbm,
                  rows_hbm, next_hbm, score_hbm, smap_hbm, rx_hbm, rg_hbm, delta_hbm, hidden_hbm,
                  xv, dyv, ids, wts, smap, sx, sg, rx, rg, wg, wu, wd, gu, delta, hid, part, b1, b2, bu, fin,
                  score, sc3, own_score, lsem, zs, zr, xs, xr, fs, fr, s1s, s1r, s2s, s2r, sus, sur, ys, yr,
                  cs, cr, es, er, ms, mr, go):
    p, i, e = place()
    z, c = e // 2, e % 2
    nz = ne // 2
    npipe = lax.axis_size("pipe")
    tokens, width = x_hbm.shape
    slots = ne * CAP
    chosen = ids.shape[0]
    hs = wg.shape[1]
    places = len(Z_PLACES)
    half = places // 2
    chip_rows = 2 * CAP
    share = half * chip_rows
    band = nd * share
    nt = (((1,), (1,)), ((), ()))
    right, left = (p, mod(i + 1, nd), e), (p, mod(i - 1, nd), e)
    sides = (right, left)
    peers = (None, right, left, (p, mod(i + 2, nd), e))
    prev, nxt = mod(p - 1, npipe), mod(p + 1, npipe)

    barrier = pltpu.get_barrier_semaphore()

    def greet(device):
        pl.semaphore_signal(barrier, inc=1, device_id=device, device_id_type=MESH)

    for d in range(1, ne):
        greet((p, i, lax.rem(e + d, ne)))
    for s in range(1, nd):
        greet(peers[s])
    greet((prev, i, e))

    loads = [pltpu.make_async_copy(a, b, lsem.at[n]) for n, (a, b) in enumerate(
        ((ids_hbm, ids), (w_hbm, wts), (x_hbm, xv), (dy_hbm, dyv), (wg_hbm, wg), (wu_hbm, wu), (wd_hbm, wd)))]
    for copy in loads:
        copy.start()
    loads[0].wait()
    loads[1].wait()

    expert, rank_of = slot_maps(ids, slots, tokens)
    hit = jnp.zeros((slots, tokens), F32)
    weight = jnp.zeros((slots, tokens), F32)
    for k in range(chosen):
        same = ids[k] == expert
        hit = jnp.where(same, 1.0, hit)
        weight = jnp.where(same, wts[k], weight)
    before = (lax.broadcasted_iota(jnp.int32, (tokens, tokens), 0)
              < lax.broadcasted_iota(jnp.int32, (tokens, tokens), 1))
    rank = jnp.dot(hit.astype(BF16), jnp.where(before, 1.0, 0.0).astype(BF16), preferred_element_type=F32)
    table = jnp.where(rank == rank_of.astype(F32), hit, 0.0)
    slot_weight = jnp.sum(table * weight, axis=1, keepdims=True)
    table = table.astype(BF16)
    smap[...] = table
    loads[2].wait()
    sx[...] = jnp.dot(table, xv[...], preferred_element_type=F32).astype(BF16)
    pl.semaphore_wait(barrier, ne - 1 + nd - 1 + 1)

    send, recv = (sx, sg), (rx, rg)

    def group(pos, slot):
        return pl.ds(pos // half * band + slot * share + pos % half * chip_rows, chip_rows)

    def core(dc):
        return c + dc - 2 * c * dc

    def z_copy(kind, pos, dc):
        target = mod(z - Z_PLACES[pos], nz) * 2 + core(dc)
        row = pos // half * band + pos % half * chip_rows
        return remote(send[kind].at[eight(target * CAP)], recv[kind].at[eight(row + c * CAP)],
                      zs.at[kind, 2 * pos + dc], zr.at[kind, 2 * pos + dc], (p, i, target))

    def own(kind):
        return pltpu.make_async_copy(send[kind].at[eight(e * CAP)], recv[kind].at[eight(c * CAP)], lsem.at[7 + kind])

    def x_copy(kind, pos, way):
        return remote(recv[kind].at[group(pos, 0)], recv[kind].at[group(pos, 2 - way)],
                      xs.at[kind, pos, way], xr.at[kind, pos, way], sides[way])

    def f_way(kind, pos):
        return (pos + kind) % 2

    def f_copy(kind, pos):
        way = f_way(kind, pos)
        return remote(recv[kind].at[group(pos, 2 - way)], recv[kind].at[group(pos, 3)],
                      fs.at[kind, pos], fr.at[kind, pos], sides[way])

    def z_send(kind, pos):
        for dc in (0, 1):
            if (pos, dc) == (0, 0):
                own(kind).start()
            else:
                z_copy(kind, pos, dc).start()

    def z_step(kind, pos):
        for dc in (0, 1):
            if (pos, dc) == (0, 0):
                own(kind).wait()
            else:
                z_copy(kind, pos, dc).wait_recv()
        for way in (0, 1):
            x_copy(kind, pos, way).start()

    def forward(kind, pos):
        x_copy(kind, pos, f_way(kind, pos)).wait_recv()
        f_copy(kind, pos).start()

    def direct_in(kind, h):
        for pos in range(h * half, (h + 1) * half):
            x_copy(kind, pos, 1 - f_way(kind, pos)).wait_recv()

    def opposite_in(kind, h):
        for pos in range(h * half, (h + 1) * half):
            f_copy(kind, pos).wait_recv()

    def map_copy():
        return remote(smap, next_hbm, ms.at[0], mr.at[0], (prev, i, e))

    def rows(h, slot, count):
        return slice(h * band + slot * share, h * band + (slot + count) * share)

    def inner(h, slot, count):
        r = rows(h, slot, count)
        gu[r, 0:hs] = jnp.dot(rx[r, :], wg[...], preferred_element_type=F32)
        gu[r, hs:] = jnp.dot(rx[r, :], wu[...], preferred_element_type=F32)

    def act(h, slot, count):
        r = rows(h, slot, count)
        n = count * share
        gate, up = gu[r, 0:hs], gu[r, hs:]
        gh = lax.dot_general(rg[r, :], wd[...], nt, preferred_element_type=F32)
        sig = jax.nn.sigmoid(gate)
        swish = gate * sig
        hidden = swish * up
        total = jnp.sum(hidden * gh, axis=1, keepdims=True)
        lane = lax.broadcasted_iota(jnp.int32, (n, 128), 1)
        row = jnp.bitwise_and(lax.broadcasted_iota(jnp.int32, (n, 128), 0), CAP - 1)
        spread = jnp.where(lane == row, jnp.broadcast_to(total, (n, 128)), 0.0)
        score[r.start // CAP:r.stop // CAP] = jnp.sum(spread.reshape(n // CAP, CAP, 128), axis=1, keepdims=True)
        hid[r, :] = hidden.astype(BF16)
        delta[r, 0:hs] = (gh * up * sig * (1.0 + gate * (1.0 - sig))).astype(BF16)
        delta[r, hs:] = (gh * swish).astype(BF16)

    def partial(h, slot, count):
        r = rows(h, slot, count)
        dg, du = delta[r, 0:hs], delta[r, hs:]
        wide = 512
        for t in range(width // wide):
            cut = slice(t * wide, (t + 1) * wide)
            value = lax.dot_general(dg, wg[cut, :], nt, preferred_element_type=F32)
            value += lax.dot_general(du, wu[cut, :], nt, preferred_element_type=F32)
            part[r, cut] = value.astype(BF16)

    def mine(h):
        return slice(h * share, (h + 1) * share)

    def cols(q):
        return slice(pieces[q][1], pieces[q][1] + pieces[q][2])

    def step1(q):
        h = pieces[q][0]
        return remote(part.at[rows(h, 3, 1), cols(q)], b1.at[mine(h), cols(q)], s1s.at[q], s1r.at[q], sides[q % 2])

    def plain(q):
        h = pieces[q][0]
        return remote(part.at[rows(h, 2 - q % 2, 1), cols(q)], bu.at[mine(h), cols(q)], sus.at[q], sur.at[q],
                      sides[1 - q % 2])

    def step2(q):
        h = pieces[q][0]
        return remote(b1.at[mine(h), cols(q)], b2.at[mine(h), cols(q)], s2s.at[q], s2r.at[q], sides[q % 2])

    def score_x(s, h):
        blocks = share // CAP
        n = (s - 1) * 2 + h
        return remote(score.at[pl.ds((h * nd + s) * blocks, blocks)], sc3.at[s - 1, pl.ds(h * blocks, blocks)],
                      cs.at[n], cr.at[n], peers[s])

    def score_z(pos, dc):
        target = mod(z + Z_PLACES[pos], nz) * 2 + core(dc)
        return remote(own_score.at[2 * pos + core(dc)], score_hbm.at[e], es.at[2 * pos + dc], er.at[2 * pos + dc],
                      (p, i, target))

    def score_own():
        return pltpu.make_async_copy(own_score.at[c], score_hbm.at[e], lsem.at[9])

    def y_copy(pair, pos, dc):
        h, start, size = pieces[2 * pair]
        wide = pl.ds(start, 2 * size)
        target = mod(z + Z_PLACES[pos], nz) * 2 + core(dc)
        n = pos % half * 2 + dc
        return remote(fin.at[eight(pos * chip_rows + core(dc) * CAP), wide], rows_hbm.at[eight(e * CAP), wide],
                      ys.at[pair, n], yr.at[pair, n], (prev, i, target))

    def all_y(pair):
        h = pieces[2 * pair][0]
        return [y_copy(pair, pos, dc) for pos in range(h * half, (h + 1) * half) for dc in (0, 1)]

    def both(copy, pair):
        for q in (2 * pair, 2 * pair + 1):
            copy(q).start()

    def middle(pair):
        for q in (2 * pair, 2 * pair + 1):
            h = pieces[q][0]
            step1(q).wait_recv()
            total = part[rows(h, 1 + q % 2, 1), cols(q)].astype(F32) + b1[mine(h), cols(q)].astype(F32)
            b1[mine(h), cols(q)] = total.astype(BF16)
            step2(q).start()

    def finish(pair):
        h = pieces[2 * pair][0]
        for q in (2 * pair, 2 * pair + 1):
            plain(q).wait_recv()
            step2(q).wait_recv()
            total = (part[rows(h, 0, 1), cols(q)].astype(F32) + b2[mine(h), cols(q)].astype(F32)
                     + bu[mine(h), cols(q)].astype(F32))
            fin[mine(h), cols(q)] = total.astype(BF16)
        for copy in all_y(pair):
            copy.start()

    first, second = len(PAIRS[0]), len(PAIRS[1])

    for pos in range(LOOK):
        z_send(0, pos)
    loads[3].wait()
    sg[...] = (slot_weight * jnp.dot(table, dyv[...], preferred_element_type=F32)).astype(BF16)
    for pos in range(LOOK):
        z_send(1, pos)
    pl.semaphore_signal(go, inc=1, device_id=(nxt, i, e), device_id_type=MESH)
    for copy in loads[4:]:
        copy.wait()
    steps = [(kind, pos) for pos in range(places) for kind in (0, 1)]
    for t, (kind, pos) in enumerate(steps):
        z_step(kind, pos)
        if kind == 1 and pos + LOOK < places:
            z_send(0, pos + LOOK)
            z_send(1, pos + LOOK)
        if t >= LAG:
            forward(*steps[t - LAG])
        if t == 13:
            direct_in(0, 0)
            opposite_in(0, 0)
            inner(0, 0, nd)
    forward(*steps[12])
    direct_in(1, 0)
    opposite_in(1, 0)
    act(0, 0, nd)
    forward(*steps[13])
    forward(*steps[14])
    partial(0, 1, nd - 1)
    forward(*steps[15])
    for pair in range(first):
        both(step1, pair)
        both(plain, pair)
    pl.semaphore_wait(go, 1)
    map_copy().start()
    partial(0, 0, 1)
    direct_in(0, 1)
    inner(1, 0, nd - 1)
    middle(0)
    direct_in(1, 1)
    act(1, 0, nd - 1)
    for pair in range(1, first):
        middle(pair)
    partial(1, 1, 2)
    both(plain, first)
    both(plain, first + 1)
    opposite_in(0, 1)
    inner(1, 3, 1)
    opposite_in(1, 1)
    act(1, 3, 1)
    partial(1, 3, 1)
    both(step1, first)
    both(step1, first + 1)
    for s in range(1, nd):
        for h in (0, 1):
            score_x(s, h).start()
    for pair in range(first):
        finish(pair)
    partial(1, 0, 1)
    middle(first)
    for pair in range(first + 2, first + second):
        both(step1, pair)
        both(plain, pair)
    middle(first + 1)
    finish(first)
    for s in range(1, nd):
        for h in (0, 1):
            score_x(s, h).wait_recv()
    blocks = share // CAP
    for h in (0, 1):
        here = slice(h * blocks, (h + 1) * blocks)
        own_score[here] = (score[h * nd * blocks:h * nd * blocks + blocks]
                           + sc3[0, here] + sc3[1, here] + sc3[2, here])
    score_own().start()
    for pos in range(places):
        for dc in (0, 1):
            if (pos, dc) != (0, 0):
                score_z(pos, dc).start()
    saves = [pltpu.make_async_copy(a, b, lsem.at[10 + n]) for n, (a, b) in enumerate(
        ((rx, rx_hbm), (rg, rg_hbm), (delta, delta_hbm), (hid, hidden_hbm), (smap, smap_hbm)))]
    for copy in saves:
        copy.start()
    for pair in range(first + 2, first + second):
        middle(pair)
        finish(pair - 1)
    finish(first + second - 1)

    for copy in saves:
        copy.wait()
    for kind in (0, 1):
        for pos in range(places):
            for dc in (0, 1):
                if (pos, dc) != (0, 0):
                    z_copy(kind, pos, dc).wait_send()
            for way in (0, 1):
                x_copy(kind, pos, way).wait_send()
            f_copy(kind, pos).wait_send()
    for q in range(len(pieces)):
        step1(q).wait_send()
        plain(q).wait_send()
        step2(q).wait_send()
    map_copy().wait_send()
    map_copy().wait_recv()
    score_own().wait()
    for s in range(1, nd):
        for h in (0, 1):
            score_x(s, h).wait_send()
    for pos in range(places):
        for dc in (0, 1):
            if (pos, dc) != (0, 0):
                score_z(pos, dc).wait_send()
                score_z(pos, dc).wait_recv()
    for pair in range(len(pieces) // 2):
        for copy in all_y(pair):
            copy.wait_send()
            copy.wait_recv()


def routed(acts, grads, ids, weights, wg, wu, wd, nd, ne):
    tokens, width = acts.shape
    hs = wg.shape[1]
    slots = ne * CAP
    rows = nd * slots
    pieces = []
    for h, sizes in enumerate(PAIRS):
        start = 0
        for size in sizes:
            pieces += [(h, start, size // 2), (h, start + size // 2, size // 2)]
            start += size
    hbm = pl.BlockSpec(memory_space=pltpu.HBM)
    dma = pltpu.SemaphoreType.DMA
    places, n = len(Z_PLACES), len(pieces)
    shape = jax.ShapeDtypeStruct
    block = pltpu.VMEM((slots, width), BF16)
    full = pltpu.VMEM((rows, width), BF16)
    return pl.pallas_call(
        functools.partial(routed_kernel, nd, ne, pieces),
        out_shape=(shape((slots, width), BF16), shape((slots, tokens), BF16), shape((ne, 1, 128), F32),
                   shape((slots, tokens), BF16), shape((rows, width), BF16), shape((rows, width), BF16),
                   shape((rows, 2 * hs), BF16), shape((rows, hs), BF16)),
        in_specs=[hbm] * 7,
        out_specs=(hbm,) * 8,
        scratch_shapes=[pltpu.VMEM((tokens, width), BF16), pltpu.VMEM((tokens, width), BF16),
                        pltpu.VMEM(ids.shape, jnp.int32), pltpu.VMEM(ids.shape, F32), pltpu.VMEM((slots, tokens), BF16),
                        block, block, full, full, pltpu.VMEM(wg.shape, BF16), pltpu.VMEM(wu.shape, BF16),
                        pltpu.VMEM(wd.shape, BF16), pltpu.VMEM((rows, 2 * hs), F32), pltpu.VMEM((rows, 2 * hs), BF16),
                        pltpu.VMEM((rows, hs), BF16), full, block, block, block, block,
                        pltpu.VMEM((nd * ne, 1, 128), F32), pltpu.VMEM((nd - 1, ne, 1, 128), F32),
                        pltpu.VMEM((ne, 1, 128), F32),
                        dma((15,)), dma((2, ne)), dma((2, ne)), dma((2, places, 2)), dma((2, places, 2)),
                        dma((2, places)), dma((2, places))] + [dma((n,))] * 6 + [dma((n // 2, ne // 2))] * 2
        + [dma((2 * (nd - 1),))] * 2 + [dma((ne,))] * 2 + [dma((1,))] * 2 + [pltpu.SemaphoreType.REGULAR],
        compiler_params=pltpu.CompilerParams(collective_id=0, has_side_effects=True, vmem_limit_bytes=VMEM_LIMIT),
        name="routed",
    )(acts, grads, ids, weights, wg, wu, wd)


def local_kernel(rx, rg, delta, hid, rows, snext, smap, score, ids_ref, w_ref, out, gwg, dwg, dwu, dwd):
    tn = (((0,), (0,)), ((), ()))
    hs = hid.shape[1]
    slots, tokens = smap.shape

    @pl.when(pl.program_id(0) == 0)
    def _():
        ne = slots // CAP
        column = jnp.broadcast_to(score[...], (ne, CAP, 128)).reshape(slots, 128)
        expert, _ = slot_maps(ids_ref, slots, tokens)
        lane = lax.broadcasted_iota(jnp.int32, (slots, 128), 1)
        row = jnp.bitwise_and(lax.broadcasted_iota(jnp.int32, (slots, 128), 0), CAP - 1)
        column = jnp.sum(jnp.where(lane == row, column, 0.0), axis=1, keepdims=True)
        spread = smap[...].astype(F32) * column
        for k in range(ids_ref.shape[0]):
            picked = jnp.sum(jnp.where(ids_ref[k] == expert, spread, 0.0), axis=0, keepdims=True)
            gwg[k] = picked / w_ref[k]

    out[...] = lax.dot_general(snext[...], rows[...], tn, preferred_element_type=F32).astype(BF16)
    both = lax.dot_general(rx[...], delta[...], tn, preferred_element_type=F32).astype(BF16)
    dwg[...] = both[:, :hs]
    dwu[...] = both[:, hs:]
    dwd[...] = lax.dot_general(hid[...], rg[...], tn, preferred_element_type=F32).astype(BF16)


def local(rows, snext, score, smap, rx, rg, delta, hid, ids, weights):
    count, width = rx.shape
    hs = hid.shape[1]
    slots, tokens = smap.shape
    wide = 512

    def whole(array):
        return pl.BlockSpec(array.shape, lambda t: (0,) * array.ndim)

    def across(height):
        return pl.BlockSpec((height, wide), lambda t: (0, t))

    down = pl.BlockSpec((wide, hs), lambda t: (t, 0))
    shape = jax.ShapeDtypeStruct
    return pl.pallas_call(
        local_kernel,
        grid=(width // wide,),
        out_shape=(shape((tokens, width), BF16), shape(ids.shape, F32), shape((width, hs), BF16),
                   shape((width, hs), BF16), shape((hs, width), BF16)),
        in_specs=[across(count), across(count), whole(delta), whole(hid), across(slots), whole(snext), whole(smap),
                  whole(score), whole(ids), whole(weights)],
        out_specs=(across(tokens), whole(ids), down, down, across(hs)),
        compiler_params=pltpu.CompilerParams(vmem_limit_bytes=VMEM_LIMIT),
        name="local",
    )(rx, rg, delta, hid, rows, snext, smap, score, ids, weights)


def shards(block_input, output_grad, expert_ids, gate_weights, gate_proj, up_proj, down_proj):
    nd, ne = lax.axis_size("dp"), lax.axis_size("expert")
    ids = jnp.transpose(expert_ids, (2, 0, 1))
    weights = jnp.transpose(gate_weights, (2, 0, 1))
    outs = routed(block_input[0], output_grad[0], ids, weights, gate_proj[0, 0], up_proj[0, 0], down_proj[0, 0],
                  nd, ne)
    received, gwg, dwg, dwu, dwd = local(*outs, ids, weights)
    return (received[None], jnp.transpose(gwg, (1, 2, 0)), dwg[None, None], dwu[None, None], dwd[None, None])


def solution(mesh):
    in_specs = (
        P("pipe", ("dp", "expert"), None),
        P("pipe", ("dp", "expert"), None),
        P("pipe", ("dp", "expert"), None),
        P("pipe", ("dp", "expert"), None),
        P("pipe", "expert", None, "dp"),
        P("pipe", "expert", None, "dp"),
        P("pipe", "expert", "dp", None),
    )
    out_specs = (
        P("pipe", ("dp", "expert"), None),
        P("pipe", ("dp", "expert"), None),
        P("pipe", "expert", None, "dp"),
        P("pipe", "expert", None, "dp"),
        P("pipe", "expert", "dp", None),
    )
    return jax.shard_map(shards, mesh=mesh, in_specs=in_specs, out_specs=out_specs, check_vma=False)
```

time: 123 us -> 116 us (0.943); the launches traced: 123 us -> 114 us
  Pallas kernels: 122 us -> 114 us
    pallas_call x1, Pallas kernels: 114 us -> 106 us  [routed(): pl.pallas_call(functools.partial(routed_kernel, nd, ne, pieces), out_shap...]
where the time goes in v3:
time: 116 us; the launch traced here: 114 us
  Pallas kernels  114 us (98%)
    pallas_call x1, Pallas kernels, routed(): pl.pallas_call(functools.partial(routed_kernel, nd, ne, pieces), out_shap...  106 us
    pallas_call x1, Pallas kernels, local(): pl.pallas_call(local_kernel, grid=(width // wide,), out_shape=(shape((tok...  8.14 us

profile of v3, /device:TPU:1, one launch (start us, length us, event | category | flops | bytes accessed | tf_op | source)
XLA Modules:
  0.0 114.4 jit_solution(11301337672465248968)
XLA Ops:
  0.6 105.6 %routed.1 = (bf16[128,3072]{1,0:T(8,128)(2,1)}, bf16[128,128]{1,0:T(8,128)(2,1)}, f32[16,1,128]{2,1,0:T(1,128)}, bf16[128,128]{1,0:T(8,128)(2,1)}, bf16[512,3072...) custom-call(bf16[128,3072]{1,0:T(8,128)(2,1)} %bitcast.15, ...), custom_call_target="tpu_custom_call" | custom-call | tf_op jit(solution)/shard_map/routed/pallas_call | solution.py:404
  106.2 8.1 %local.1 = (bf16[128,3072]{1,0:T(8,128)(2,1)}, f32[6,1,128]{2,1,0:T(1,128)}, bf16[3072,256]{1,0:T(8,128)(2,1)}, bf16[3072,256]{1,0:T(8,128)(2,1)}, bf16[256,3072]{1,0:T(8,128)(2,1)}) custom-call(bf16[512,3072]{1,0:T(8,128)(2,1)} %get-tuple-element.18.rx, bf16[512,3072]{1,0:T(8,128)(2,1)} %get-tuple-element.19.rg, bf16[512,512]{1,0:T(8,128)(2,1)} %get-tuple-element.20.delta, ...), custom_call_target="tpu_custom_call" | custom-call | tf_op jit(solution)/shard_map/local/pallas_call | solution.py:465

commit v4 on v3

--- a/solution.py
+++ b/solution.py
@@ -284,52 +284,58 @@
             z_send(1, pos + LOOK)
         if t >= LAG:
             forward(*steps[t - LAG])
-        if t == 13:
+        if t == 11:
             direct_in(0, 0)
             opposite_in(0, 0)
             inner(0, 0, nd)
+        if t == 12:
+            direct_in(1, 0)
+            opposite_in(1, 0)
+            act(0, 0, nd)
+        if t == 14:
+            partial(0, 3, 1)
+            for pair in range(first):
+                both(step1, pair)
     forward(*steps[12])
-    direct_in(1, 0)
-    opposite_in(1, 0)
-    act(0, 0, nd)
     forward(*steps[13])
+    partial(0, 1, 2)
     forward(*steps[14])
-    partial(0, 1, nd - 1)
     forward(*steps[15])
-    for pair in range(first):
-        both(step1, pair)
+    middle(0)
+    both(plain, 0)
+    for pair in range(1, first):
+        middle(pair)
         both(plain, pair)
     pl.semaphore_wait(go, 1)
     map_copy().start()
     partial(0, 0, 1)
     direct_in(0, 1)
     inner(1, 0, nd - 1)
-    middle(0)
+    opposite_in(0, 1)
+    inner(1, 3, 1)
     direct_in(1, 1)
     act(1, 0, nd - 1)
-    for pair in range(1, first):
-        middle(pair)
-    partial(1, 1, 2)
-    both(plain, first)
-    both(plain, first + 1)
-    opposite_in(0, 1)
-    inner(1, 3, 1)
     opposite_in(1, 1)
     act(1, 3, 1)
     partial(1, 3, 1)
-    both(step1, first)
-    both(step1, first + 1)
+    for pair in range(first, first + second):
+        both(step1, pair)
+    partial(1, 1, 2)
+    both(plain, first)
     for s in range(1, nd):
         for h in (0, 1):
             score_x(s, h).start()
+    saves = [pltpu.make_async_copy(a, b, lsem.at[10 + n]) for n, (a, b) in enumerate(
+        ((rx, rx_hbm), (rg, rg_hbm), (delta, delta_hbm), (hid, hidden_hbm), (smap, smap_hbm)))]
+    for copy in saves:
+        copy.start()
+    partial(1, 0, 1)
     for pair in range(first):
         finish(pair)
-    partial(1, 0, 1)
-    middle(first)
-    for pair in range(first + 2, first + second):
-        both(step1, pair)
-        both(plain, pair)
-    middle(first + 1)
+    for pair in range(first, first + second):
+        middle(pair)
+        if pair + 1 < first + second:
+            both(plain, pair + 1)
     finish(first)
     for s in range(1, nd):
         for h in (0, 1):
@@ -344,14 +350,8 @@
         for dc in (0, 1):
             if (pos, dc) != (0, 0):
                 score_z(pos, dc).start()
-    saves = [pltpu.make_async_copy(a, b, lsem.at[10 + n]) for n, (a, b) in enumerate(
-        ((rx, rx_hbm), (rg, rg_hbm), (delta, delta_hbm), (hid, hidden_hbm), (smap, smap_hbm)))]
-    for copy in saves:
-        copy.start()
-    for pair in range(first + 2, first + second):
-        middle(pair)
-        finish(pair - 1)
-    finish(first + second - 1)
+    for pair in range(first + 1, first + second):
+        finish(pair)
 
     for copy in saves:
         copy.wait()
@@ -452,7 +452,7 @@
     count, width = rx.shape
     hs = hid.shape[1]
     slots, tokens = smap.shape
-    wide = 512
+    wide = 768
 
     def whole(array):
         return pl.BlockSpec(array.shape, lambda t: (0,) * array.ndim)

time: 116 us -> 114 us (0.983); the launches traced: 114 us -> 114 us
  no operation moved by 1% of the time
where the time goes in v4:
time: 114 us
  Pallas kernels  113 us (99%)
    pallas_call x1, Pallas kernels, routed(): pl.pallas_call(functools.partial(routed_kernel, nd, ne, pieces), out_shap...  106 us
    pallas_call x1, Pallas kernels, local(): pl.pallas_call(local_kernel, grid=(width // wide,), out_shape=(shape((tok...  7.45 us

profile of v4, /device:TPU:1, one launch (start us, length us, event | category | flops | bytes accessed | tf_op | source)
XLA Modules:
  0.0 113.9 jit_solution(5204386151216088384)
XLA Ops:
  0.6 105.8 %routed.1 = (bf16[128,3072]{1,0:T(8,128)(2,1)}, bf16[128,128]{1,0:T(8,128)(2,1)}, f32[16,1,128]{2,1,0:T(1,128)}, bf16[128,128]{1,0:T(8,128)(2,1)}, bf16[512,3072...) custom-call(bf16[128,3072]{1,0:T(8,128)(2,1)} %bitcast.15, ...), custom_call_target="tpu_custom_call" | custom-call | tf_op jit(solution)/shard_map/routed/pallas_call | solution.py:404
  106.5 7.5 %local.1 = (bf16[128,3072]{1,0:T(8,128)(2,1)}, f32[6,1,128]{2,1,0:T(1,128)}, bf16[3072,256]{1,0:T(8,128)(2,1)}, bf16[3072,256]{1,0:T(8,128)(2,1)}, bf16[256,3072]{1,0:T(8,128)(2,1)}) custom-call(bf16[512,3072]{1,0:T(8,128)(2,1)} %get-tuple-element.18.rx, bf16[512,3072]{1,0:T(8,128)(2,1)} %get-tuple-element.19.rg, bf16[512,512]{1,0:T(8,128)(2,1)} %get-tuple-element.20.delta, ...), custom_call_target="tpu_custom_call" | custom-call | tf_op jit(solution)/shard_map/local/pallas_call | solution.py:465

commit v5 on v4

--- a/solution.py
+++ b/solution.py
@@ -11,7 +11,7 @@
 F32 = jnp.float32
 BF16 = jnp.bfloat16
 VMEM_LIMIT = 58 << 20
-Z_PLACES = (0, 1, -1, 2, -2, 3, -3, 4)
+Z_PLACES = (0, 1, -1, 4, 2, -2, 3, -3)
 LOOK = 2
 LAG = 4
 PAIRS = ((1536, 1536), (1280, 1024, 768))

time: 114 us -> 113 us (level)
  no operation moved by 1% of the time
where the time goes in v5:
time: 113 us
  Pallas kernels  113 us (100%)
    pallas_call x1, Pallas kernels, routed(): pl.pallas_call(functools.partial(routed_kernel, nd, ne, pieces), out_shap...  105 us
    pallas_call x1, Pallas kernels, local(): pl.pallas_call(local_kernel, grid=(width // wide,), out_shape=(shape((tok...  7.45 us

profile of v5, /device:TPU:1, one launch (start us, length us, event | category | flops | bytes accessed | tf_op | source)
XLA Modules:
  0.0 113.2 jit_solution(13058962334571932992)
XLA Ops:
  0.6 105.1 %routed.1 = (bf16[128,3072]{1,0:T(8,128)(2,1)}, bf16[128,128]{1,0:T(8,128)(2,1)}, f32[16,1,128]{2,1,0:T(1,128)}, bf16[128,128]{1,0:T(8,128)(2,1)}, bf16[512,3072...) custom-call(bf16[128,3072]{1,0:T(8,128)(2,1)} %bitcast.15, ...), custom_call_target="tpu_custom_call" | custom-call | tf_op jit(solution)/shard_map/routed/pallas_call | solution.py:404
  105.8 7.5 %local.1 = (bf16[128,3072]{1,0:T(8,128)(2,1)}, f32[6,1,128]{2,1,0:T(1,128)}, bf16[3072,256]{1,0:T(8,128)(2,1)}, bf16[3072,256]{1,0:T(8,128)(2,1)}, bf16[256,3072]{1,0:T(8,128)(2,1)}) custom-call(bf16[512,3072]{1,0:T(8,128)(2,1)} %get-tuple-element.18.rx, bf16[512,3072]{1,0:T(8,128)(2,1)} %get-tuple-element.19.rg, bf16[512,512]{1,0:T(8,128)(2,1)} %get-tuple-element.20.delta, ...), custom_call_target="tpu_custom_call" | custom-call | tf_op jit(solution)/shard_map/local/pallas_call | solution.py:465
